TPU v7x, 1024 devices: a whole 8x8x8 slice. The times are simulated.
1024 devices in a mesh: gx: 16 (over x, core), gy: 64 (over z, y).
Axes of the slice: x: 8, y: 8, z: 8, core: 2. Of those that a mesh axis runs over, the one named last changes fastest.
Arguments:
- stream_vel: float32 [512, 16, 2048], P('gy', None, 'gx'), may hold values from -6 to 6
- normal_vel: float32 [512, 16, 2048], P('gy', None, 'gx'), may hold values from -6 to 6
- span_vel: float32 [512, 16, 2048], P('gy', None, 'gx'), may hold values from -6 to 6
Outputs:
- pressure: float32 [512, 16, 2048], P('gy', None, 'gx')
- stream_next: float32 [512, 16, 2048], P('gy', None, 'gx')
- normal_next: float32 [512, 16, 2048], P('gy', None, 'gx')
- span_next: float32 [512, 16, 2048], P('gy', None, 'gx')
All inputs are finite; a program needn't handle non-finite values.
Results may differ from a plain program's by a relative error of at most 0.0004.
Values sent between devices are 32-bit elements; how exact they have to be, the bound alone decides.
No kernel may reach another device: no remote copies, remote signals or barrier semaphores. Data moves between devices by JAX's collectives and lax.ppermute only.
A program may use at most 32 MiB of HBM per device.

v0:
```python
import math

import jax
import jax.numpy as jnp
from jax import lax
from jax.sharding import PartitionSpec as P

shift_term = 1.0 / 1024.0
grid_ratio = 1.0 / 128.0
highest = lax.Precision.HIGHEST


def padded(block, sides, width):
    for axis, dim in sides:
        count = lax.axis_size(axis)
        forward = [(i, i + 1) for i in range(count - 1)]
        forward.append((count - 1, 0))
        backward = [(target, source) for source, target in forward]
        low = lax.ppermute(
            lax.slice_in_dim(block, block.shape[dim] - width, None, axis=dim), axis, forward
        )
        high = lax.ppermute(lax.slice_in_dim(block, 0, width, axis=dim), axis, backward)
        block = jnp.concatenate([low, block, high], axis=dim)
    return block


def from_partner(array, axis, bit):
    return lax.ppermute(array, axis, [(i, i ^ 1 << bit) for i in range(lax.axis_size(axis))])


def entering(value, axis, join, neutral, backward):
    count, mine = (lax.axis_size(axis), lax.axis_index(axis))
    pieces = jax.tree.map(lambda part: lax.all_gather(part, axis), value)
    if backward:
        pieces = jax.tree.map(lambda part: part[::-1], pieces)
        mine = count - 1 - mine
    subtotal = jax.tree.map(
        lambda part, zero: jnp.full_like(part, 0) + jnp.asarray(zero, part.dtype), value, neutral
    )

    def hop(position, subtotal):
        longer = join(subtotal, jax.tree.map(lambda part: part[position], pieces))
        return jax.tree.map(lambda new, old: jnp.where(position < mine, new, old), longer, subtotal)

    return lax.fori_loop(0, count - 1, hop, subtotal)


def padded_rims(stacked):
    return padded(stacked, (("gx", 3), ("gy", 1)), 1)


def partner_block(grid_data, level_bit):
    return from_partner(grid_data, "gx", level_bit)


def dft_tables(length):
    index_row = jnp.arange(length, dtype=jnp.int32)
    product = index_row[:, None] * index_row[None, :] % length
    phase_table = 2.0 * math.pi / length * product.astype(jnp.float32)
    return (jnp.cos(phase_table), jnp.sin(phase_table))


def rotated(grid_data, phase_angle):
    cosine = jnp.cos(phase_angle)
    sine = jnp.sin(phase_angle)
    return jnp.stack(
        [grid_data[0] * cosine - grid_data[1] * sine, grid_data[0] * sine + grid_data[1] * cosine]
    )


def along_last(grid_data, cosines, sines, sign_value):
    cos_all = jnp.einsum("...i,ik->...k", grid_data, cosines, precision=highest)
    sin_all = jnp.einsum("...i,ik->...k", grid_data, sines, precision=highest)
    return jnp.stack([cos_all[0] - sign_value * sin_all[1], cos_all[1] + sign_value * sin_all[0]])


def reversed_bits(position, bit_count):
    reversed_value = jnp.zeros((), jnp.int32)
    for bit_place in range(bit_count):
        picked = jnp.bitwise_and(jnp.right_shift(position, bit_place), 1)
        reversed_value = reversed_value + picked * (1 << bit_count - 1 - bit_place)
    return reversed_value


def butterfly_forward(grid_data, position, bit_count):
    for section_index in range(bit_count):
        level_bit = bit_count - 1 - section_index
        half_span = 1 << level_bit
        partner = partner_block(grid_data, level_bit)
        is_upper = jnp.bitwise_and(jnp.right_shift(position, level_bit), 1)
        offset = jnp.bitwise_and(position, half_span - 1)
        phase_angle = -math.pi / half_span * offset.astype(jnp.float32)
        summed = grid_data + partner
        turned = rotated(partner - grid_data, phase_angle)
        grid_data = jnp.where(is_upper == 1, turned, summed)
    return grid_data


def butterfly_inverse(grid_data, position, bit_count):
    for level_bit in range(bit_count):
        half_span = 1 << level_bit
        partner = partner_block(grid_data, level_bit)
        is_upper = jnp.bitwise_and(jnp.right_shift(position, level_bit), 1)
        offset = jnp.bitwise_and(position, half_span - 1)
        phase_angle = math.pi / half_span * offset.astype(jnp.float32)
        lower_result = 0.5 * (grid_data + rotated(partner, phase_angle))
        upper_result = 0.5 * (partner - rotated(grid_data, phase_angle))
        grid_data = jnp.where(is_upper == 1, upper_result, lower_result)
    return grid_data


def spread_modes(grid_data, mode_first, length_x, parts_x, cos_x, sin_x):
    cells_x = grid_data.shape[-1]
    cell_x = jnp.arange(cells_x, dtype=jnp.int32)
    twist = -2.0 * math.pi / length_x * (cell_x * mode_first).astype(jnp.float32)
    grid_data = rotated(grid_data, twist)
    grid_data = along_last(grid_data, cos_x, sin_x, -1.0)
    mode_x = mode_first + parts_x * cell_x
    return (grid_data, twist, mode_x)


def chain_forward(inner_map, outer_map):
    top_left = outer_map[0] * inner_map[0] + outer_map[1] * inner_map[2]
    top_right = outer_map[0] * inner_map[1] + outer_map[1] * inner_map[3]
    low_left = outer_map[2] * inner_map[0] + outer_map[3] * inner_map[2]
    low_right = outer_map[2] * inner_map[1] + outer_map[3] * inner_map[3]
    carry_gain = outer_map[4] * inner_map[4]
    feeds = []
    for offset_index in (5, 7):
        feeds.append(
            outer_map[4] * inner_map[offset_index]
            + outer_map[offset_index] * inner_map[0]
            + outer_map[offset_index + 1] * inner_map[2]
        )
        feeds.append(
            outer_map[4] * inner_map[offset_index + 1]
            + outer_map[offset_index] * inner_map[1]
            + outer_map[offset_index + 1] * inner_map[3]
        )
    scale_value = jnp.maximum(
        jnp.maximum(jnp.abs(top_left), jnp.abs(top_right)),
        jnp.maximum(jnp.abs(low_left), jnp.abs(low_right)),
    )
    entries = (
        top_left,
        top_right,
        low_left,
        low_right,
        carry_gain,
        feeds[0],
        feeds[1],
        feeds[2],
        feeds[3],
    )
    return tuple((entry / scale_value for entry in entries))


def chain_back(inner_map, outer_map):
    return (
        outer_map[0] * inner_map[0],
        outer_map[1] + outer_map[0] * inner_map[1],
        outer_map[2] + outer_map[0] * inner_map[2],
    )


def solve_modes(grid_data, centre, row_global, length_y):
    below_coef = jnp.where(row_global == 0, jnp.float32(0.0), jnp.float32(1.0))
    above_coef = jnp.where(row_global == length_y - 1, jnp.float32(0.0), jnp.float32(1.0))
    end_extra = 1.0 - below_coef + (1.0 - above_coef)
    zeros_map = jnp.zeros_like(centre)
    ones_map = jnp.ones_like(centre)
    row_inputs_all = (below_coef, above_coef, end_extra, grid_data[0], grid_data[1])

    def compose_row(carry_map, row_inputs):
        lower_c, upper_c, extra_c, right_re, right_im = row_inputs
        row_map = (
            zeros_map,
            upper_c * ones_map,
            -lower_c * ones_map,
            centre + extra_c,
            -lower_c * ones_map,
            zeros_map,
            right_re,
            zeros_map,
            right_im,
        )
        return (chain_forward(carry_map, row_map), None)

    identity_map = (
        ones_map,
        zeros_map,
        zeros_map,
        ones_map,
        ones_map,
        zeros_map,
        zeros_map,
        zeros_map,
        zeros_map,
    )
    local_map, _ = lax.scan(compose_row, identity_map, row_inputs_all)
    incoming = entering(local_map, "gy", chain_forward, identity_map, False)
    start_ratio = incoming[1] / incoming[3]
    start_re = incoming[6] / incoming[3]
    start_im = incoming[8] / incoming[3]

    def eliminate(carry_state, row_inputs):
        lower_c, upper_c, extra_c, right_re, right_im = row_inputs
        pivot = centre + extra_c - lower_c * carry_state[0]
        ratio_next = upper_c / pivot
        value_re = (right_re - lower_c * carry_state[1]) / pivot
        value_im = (right_im - lower_c * carry_state[2]) / pivot
        return ((ratio_next, value_re, value_im), (ratio_next, value_re, value_im))

    _, (ratios, values_re, values_im) = lax.scan(
        eliminate, (start_ratio, start_re, start_im), row_inputs_all
    )

    def back_row(carry_map, row_inputs):
        ratio_row, value_re, value_im = row_inputs
        return (chain_back(carry_map, (-ratio_row, value_re, value_im)), None)

    back_identity = (ones_map, zeros_map, zeros_map)
    local_back, _ = lax.scan(back_row, back_identity, (ratios, values_re, values_im), reverse=True)
    incoming_back = entering(local_back, "gy", chain_back, back_identity, True)

    def substitute(carry_state, row_inputs):
        ratio_row, value_re, value_im = row_inputs
        solved_re = value_re - ratio_row * carry_state[0]
        solved_im = value_im - ratio_row * carry_state[1]
        return ((solved_re, solved_im), (solved_re, solved_im))

    _, (press_re, press_im) = lax.scan(
        substitute,
        (incoming_back[1], incoming_back[2]),
        (ratios, values_re, values_im),
        reverse=True,
    )
    return jnp.stack([press_re, press_im])


def per_device(stream_vel, normal_vel, span_vel):
    rows_dev, planes, cells_x = stream_vel.shape
    parts_x = lax.axis_size("gx")
    parts_y = lax.axis_size("gy")
    where_x = lax.axis_index("gx")
    where_y = lax.axis_index("gy")
    length_x = cells_x * parts_x
    length_y = rows_dev * parts_y
    bit_count = parts_x.bit_length() - 1
    row_local = jnp.arange(rows_dev, dtype=jnp.int32)
    row_global = where_y * rows_dev + row_local
    wall_keep = jnp.where(row_global == length_y - 1, jnp.float32(0.0), jnp.float32(1.0))[
        :, None, None
    ]
    bottom_keep = jnp.where(row_global > 0, jnp.float32(1.0), jnp.float32(0.0))[:, None, None]
    normal_wall = normal_vel * wall_keep
    rimmed = padded_rims(jnp.stack([stream_vel, normal_wall]))
    stream_left = rimmed[0, 1:-1, :, :-2]
    normal_below = rimmed[1, :-2, :, 1:-1] * bottom_keep
    source = (
        grid_ratio * (stream_vel - stream_left)
        + (normal_wall - normal_below)
        + grid_ratio * (span_vel - jnp.roll(span_vel, 1, axis=1))
    )
    cos_z, sin_z = dft_tables(planes)
    cos_x, sin_x = dft_tables(cells_x)
    grid_data = jnp.stack(
        [
            jnp.einsum("yzx,zk->ykx", source, cos_z, precision=highest),
            -jnp.einsum("yzx,zk->ykx", source, sin_z, precision=highest),
        ]
    )
    grid_data = butterfly_forward(grid_data, where_x, bit_count)
    mode_first = reversed_bits(where_x, bit_count)
    grid_data, twist, mode_x = spread_modes(grid_data, mode_first, length_x, parts_x, cos_x, sin_x)
    mode_z = jnp.arange(planes, dtype=jnp.int32)[:, None]
    wave_x = (2.0 * jnp.sin(math.pi * mode_x.astype(jnp.float32) / length_x)) ** 2
    wave_z = (2.0 * jnp.sin(math.pi * mode_z.astype(jnp.float32) / planes)) ** 2
    eigen_sum = grid_ratio * grid_ratio * (wave_z + wave_x) + shift_term
    centre = -(2.0 + eigen_sum)
    grid_data = solve_modes(grid_data, centre, row_global, length_y)
    grid_data = along_last(grid_data, cos_x, sin_x, 1.0) / cells_x
    grid_data = rotated(grid_data, -twist)
    grid_data = butterfly_inverse(grid_data, where_x, bit_count)
    pressure = (
        jnp.einsum("ykx,kz->yzx", grid_data[0], cos_z, precision=highest)
        - jnp.einsum("ykx,kz->yzx", grid_data[1], sin_z, precision=highest)
    ) / planes
    rimmed_p = padded_rims(pressure[None])
    stream_next = stream_vel - grid_ratio * (rimmed_p[0, 1:-1, :, 2:] - pressure)
    normal_next = (normal_vel - (rimmed_p[0, 2:, :, 1:-1] - pressure)) * wall_keep
    span_next = span_vel - grid_ratio * (jnp.roll(pressure, -1, axis=1) - pressure)
    return (pressure, stream_next, normal_next, span_next)


def solution(mesh):
    return jax.shard_map(
        per_device,
        mesh=mesh,
        in_specs=(P("gy", None, "gx"), P("gy", None, "gx"), P("gy", None, "gx")),
        out_specs=(
            P("gy", None, "gx"),
            P("gy", None, "gx"),
            P("gy", None, "gx"),
            P("gy", None, "gx"),
        ),
        check_vma=False,
    )
```

profile of v0, /device:TPU:1, one launch (start us, length us, event | category | flops | bytes accessed | tf_op | source)
XLA Modules:
  0.0 990.1 jit_solution(13990770162183363707)
XLA Ops:
  4.3 11.6 %collective-permute-start.1 = (f32[2,8,16,1]{3,2,1,0:T(8,128)S(1)}, f32[2,8,16,1]{3,2,1,0:T(8,128)S(1)}, u32[]{:S(2)}, u32[]{:S(2)}) collective-permute-start(f32[2,8,16,1]{3,2,1,0:T(8,128)S(1)} %get-tuple-element.1300), channel_id=1, source_target_pairs={{64,0},{128,64},{192,128},{256,192},{320,256},{384,320},{448,384},... | collective-permute-start | bytes 3080 | tf_op jit(solution)/shard_map/ppermute | solution.py:22
  19.0 12.2 %collective-permute-done.2 = f32[2,1,16,130]{3,2,1,0:T(8,128)S(1)} collective-permute-done((f32[2,1,16,130]{3,2,1,0:T(8,128)S(1)}, f32[2,1,16,130]{3,2,1,0:T(8,128)S(1)}, u32[]{:S(2)}, u32[]{:S(2)}) %collective-permute-start.2) | collective-permute-done | bytes 16672 | tf_op jit(solution)/shard_map/ppermute | solution.py:19
  31.8 6.2 collective-permute-start.3
  42.1 7.4 collective-permute-start.4
  49.7 5.9 collective-permute-done.4
  68.8 41.8 %while.129 = (s32[]{:T(128)}, f32[16,128]{1,0:T(8,128)S(1)}, f32[16,128]{1,0:T(8,128)S(1)}, f32[16,128]{1,0:T(8,128)S(1)}, f32[16,128]{1,0:T(8,128)S(1)}, /*inde...) while((s32[]{:T(128)}, f32[16,128]{1,0:T(8,128)S(1)}, ...), condition=%wide.region_1.2_spmd.clone, body=%wide.region_0.1_spmd.clone.sunk | while | flops 163844 | bytes 222596 | solution.py:200
  110.6 35.6 %all-gather = f32[1024,128]{1,0:T(8,128)S(1)} all-gather(f32[16,128]{1,0:T(8,128)S(1)} %get-tuple-element.869), channel_id=2, replica_groups=mesh['gx'=16,'gy'=64] {'gy'}, dimensions={0}, use_global_device_ids=true | all-gather | bytes 532480 | tf_op jit(solution)/shard_map/all_gather | solution.py:33
  146.3 35.9 %all-gather.1 = f32[1024,128]{1,0:T(8,128)S(1)} all-gather(f32[16,128]{1,0:T(8,128)S(1)} %get-tuple-element.870), channel_id=3, replica_groups=mesh['gx'=16,'gy'=64] {'gy'}, dimensions={0}, use_global_device_ids=true | all-gather | bytes 532480 | tf_op jit(solution)/shard_map/all_gather | solution.py:33
  182.3 35.9 %all-gather.2 = f32[1024,128]{1,0:T(8,128)S(1)} all-gather(f32[16,128]{1,0:T(8,128)S(1)} %get-tuple-element.871), channel_id=4, replica_groups=mesh['gx'=16,'gy'=64] {'gy'}, dimensions={0}, use_global_device_ids=true | all-gather | bytes 532480 | tf_op jit(solution)/shard_map/all_gather | solution.py:33
  218.2 35.0 %all-gather.3 = f32[1024,128]{1,0:T(8,128)S(1)} all-gather(f32[16,128]{1,0:T(8,128)S(1)} %get-tuple-element.872), channel_id=5, replica_groups=mesh['gx'=16,'gy'=64] {'gy'}, dimensions={0}, use_global_device_ids=true | all-gather | bytes 532480 | tf_op jit(solution)/shard_map/all_gather | solution.py:33
  253.3 36.3 %all-gather.4 = f32[1024,128]{1,0:T(8,128)S(1)} all-gather(f32[16,128]{1,0:T(8,128)S(1)} %get-tuple-element.873), channel_id=6, replica_groups=mesh['gx'=16,'gy'=64] {'gy'}, dimensions={0}, use_global_device_ids=true | all-gather | bytes 532480 | tf_op jit(solution)/shard_map/all_gather | solution.py:33
  289.6 35.7 %all-gather.5 = f32[1024,128]{1,0:T(8,128)S(1)} all-gather(f32[16,128]{1,0:T(8,128)S(1)} %copy-done.8), channel_id=7, replica_groups=mesh['gx'=16,'gy'=64] {'gy'}, dimensions={0}, use_global_device_ids=true | all-gather | bytes 532480 | tf_op jit(solution)/shard_map/all_gather | solution.py:33
  325.3 40.3 %all-gather.6 = f32[1024,128]{1,0:T(8,128)} all-gather(f32[16,128]{1,0:T(8,128)S(1)} %copy-done.10), channel_id=8, replica_groups=mesh['gx'=16,'gy'=64] {'gy'}, dimensions={0}, use_global_device_ids=true | all-gather | bytes 532480 | tf_op jit(solution)/shard_map/all_gather | solution.py:33
  365.6 39.0 %all-gather.7 = f32[1024,128]{1,0:T(8,128)} all-gather(f32[16,128]{1,0:T(8,128)S(1)} %copy-done.12), channel_id=9, replica_groups=mesh['gx'=16,'gy'=64] {'gy'}, dimensions={0}, use_global_device_ids=true | all-gather | bytes 532480 | tf_op jit(solution)/shard_map/all_gather | solution.py:33
  404.6 40.7 %all-gather.8 = f32[1024,128]{1,0:T(8,128)} all-gather(f32[16,128]{1,0:T(8,128)S(1)} %copy-done.14), channel_id=10, replica_groups=mesh['gx'=16,'gy'=64] {'gy'}, dimensions={0}, use_global_device_ids=true | all-gather | bytes 532480 | tf_op jit(solution)/shard_map/all_gather | solution.py:33
  445.3 211.2 %while.130 = (s32[]{:T(128)}, f32[16,128]{1,0:T(8,128)S(1)}, f32[16,128]{1,0:T(8,128)S(1)}, f32[16,128]{1,0:T(8,128)S(1)}, f32[16,128]{1,0:T(8,128)S(1)}, /*inde...) while((s32[]{:T(128)}, f32[16,128]{1,0:T(8,128)S(1)}, ...), condition=%wide.region_3.4_spmd.clone, body=%wide.region_2.3_spmd.clone.sunk | while | flops 104452 | bytes 360707 | solution.py:45
  658.0 31.4 %while.128 = (s32[]{:T(128)}, f32[16,128]{1,0:T(8,128)S(1)}, f32[16,128]{1,0:T(8,128)S(1)}, f32[16,128]{1,0:T(8,128)S(1)}, f32[8,16,128]{2,1,0:T(8,128)S(1)}, /*...) while((s32[]{:T(128)}, f32[16,128]{1,0:T(8,128)S(1)}, ...), condition=%wide.region_5.6_spmd.clone, body=%wide.region_4.5_spmd.clone.sunk | while | flops 28674 | bytes 91329 | solution.py:214
  689.7 34.7 %all-gather.10 = f32[1024,128]{1,0:T(8,128)S(1)} all-gather(f32[16,128]{1,0:T(8,128)S(1)} %get-tuple-element.886), channel_id=12, replica_groups=mesh['gx'=16,'gy'=64] {'gy'}, dimensions={0}, use_global_device_ids=true | all-gather | bytes 532480 | tf_op jit(solution)/shard_map/all_gather | solution.py:33
  724.4 36.0 %all-gather.11 = f32[1024,128]{1,0:T(8,128)S(1)} all-gather(f32[16,128]{1,0:T(8,128)S(1)} %get-tuple-element.887), channel_id=13, replica_groups=mesh['gx'=16,'gy'=64] {'gy'}, dimensions={0}, use_global_device_ids=true | all-gather | bytes 532480 | tf_op jit(solution)/shard_map/all_gather | solution.py:33
  760.5 34.7 %all-gather.9 = f32[1024,128]{1,0:T(8,128)S(1)} all-gather(f32[16,128]{1,0:T(8,128)S(1)} %get-tuple-element.885), channel_id=11, replica_groups=mesh['gx'=16,'gy'=64] {'gy'}, dimensions={0}, use_global_device_ids=true | all-gather | bytes 532480 | tf_op jit(solution)/shard_map/all_gather | solution.py:33
  799.9 148.1 %collective-permute-start.7 = (f32[2,8,16,128]{3,2,1,0:T(8,128)S(1)}, f32[2,8,16,128]{3,2,1,0:T(8,128)S(1)}, u32[]{:S(2)}, u32[]{:S(2)}) collective-permute-start(f32[2,8,16,128]{3,2,1,0:T(8,128)S(1)} %pad_maximum_fusion.4), channel_id=1, source_target_pairs={{0,64},{64,0},{128,192},{192,128},{256,320},{320,256},{384,448},{4... | collective-permute-start | bytes 393224 | tf_op jit(solution)/shard_map/ppermute | solution.py:28
  950.9 4.7 collective-permute-done.8
  958.6 8.1 collective-permute-done.9
  970.7 9.0 collective-permute-done.10
  (690 shorter events, 329.2 us)
Async XLA Ops:
  1.7 15.0 %collective-permute-start = (f32[2,8,16,1]{3,2,1,0:T(8,128)S(1)}, f32[2,8,16,1]{3,2,1,0:T(8,128)S(1)}, u32[]{:S(2)}, u32[]{:S(2)}) collective-permute-start(f32[2,8,16,1]{3,2,1,0:T(8,128)S(1)} %get-tuple-element.1299), channel_id=1, source_target_pairs={{0,64},{64,128},{128,192},{192,256},{256,320},{320,384},{384,448},... | collective-permute-start | bytes 3080 | tf_op jit(solution)/shard_map/ppermute | solution.py:19
  4.3 12.6 %collective-permute-start.1 = (f32[2,8,16,1]{3,2,1,0:T(8,128)S(1)}, f32[2,8,16,1]{3,2,1,0:T(8,128)S(1)}, u32[]{:S(2)}, u32[]{:S(2)}) collective-permute-start(f32[2,8,16,1]{3,2,1,0:T(8,128)S(1)} %get-tuple-element.1300), channel_id=1, source_target_pairs={{64,0},{128,64},{192,128},{256,192},{320,256},{384,320},{448,384},... | collective-permute-start | bytes 3080 | tf_op jit(solution)/shard_map/ppermute | solution.py:22
  17.0 14.2 %collective-permute-start.2 = (f32[2,1,16,130]{3,2,1,0:T(8,128)S(1)}, f32[2,1,16,130]{3,2,1,0:T(8,128)S(1)}, u32[]{:S(2)}, u32[]{:S(2)}) collective-permute-start(f32[2,1,16,130]{3,2,1,0:T(8,128)S(1)} %pad_maximum_fusion.19), channel_id=1, source_target_pairs={{0,1},{1,2},{2,3},{3,4},{4,5},{5,6},{6,7},{7,8},{8,9},{9,10},{10,1... | collective-permute-start | bytes 49928 | tf_op jit(solution)/shard_map/ppermute | solution.py:19
  31.8 10.1 %collective-permute-start.3 = (f32[2,8,16,128]{3,2,1,0:T(8,128)S(1)}, f32[2,8,16,128]{3,2,1,0:T(8,128)S(1)}, u32[]{:S(2)}, u32[]{:S(2)}) collective-permute-start(f32[2,8,16,128]{3,2,1,0:T(8,128)S(1)} %pad_maximum_fusion.1), channel_id=1, source_target_pairs={{0,512},{64,576},{128,640},{192,704},{256,768},{320,832},{384,896}... | collective-permute-start | bytes 393224 | tf_op jit(solution)/shard_map/ppermute | solution.py:28
  42.1 13.5 %collective-permute-start.4 = (f32[2,8,16,128]{3,2,1,0:T(8,128)S(1)}, f32[2,8,16,128]{3,2,1,0:T(8,128)S(1)}, u32[]{:S(2)}, u32[]{:S(2)}) collective-permute-start(f32[2,8,16,128]{3,2,1,0:T(8,128)S(1)} %maximum_select_fusion), channel_id=1, source_target_pairs={{0,256},{64,320},{128,384},{192,448},{256,0},{320,64},{384,128},{4... | collective-permute-start | bytes 393224 | tf_op jit(solution)/shard_map/ppermute | solution.py:28
  55.7 5.7 collective-permute-start.5
  61.5 6.1 collective-permute-start.6
  110.5 35.7 %copy-start.11 = (f32[16,128]{1,0:T(8,128)}, f32[16,128]{1,0:T(8,128)S(1)}, u32[]{:S(2)}) copy-start(f32[16,128]{1,0:T(8,128)S(1)} %get-tuple-element.876) | copy-start | bytes 24580
  110.5 35.7 %copy-start.13 = (f32[16,128]{1,0:T(8,128)}, f32[16,128]{1,0:T(8,128)S(1)}, u32[]{:S(2)}) copy-start(f32[16,128]{1,0:T(8,128)S(1)} %get-tuple-element.877) | copy-start | bytes 24580
  110.6 35.7 %copy-start.17 = (f32[16]{0:T(128)}, f32[16]{0:T(128)S(1)}, u32[]{:S(2)}) copy-start(f32[16]{0:T(128)S(1)} %get-tuple-element.2084) | copy-start | bytes 196
  110.6 35.7 %copy-start.19 = (f32[128]{0:T(128)}, f32[128]{0:T(128)S(1)}, u32[]{:S(2)}) copy-start(f32[128]{0:T(128)S(1)} %get-tuple-element.2085) | copy-start | bytes 1540
  110.6 35.7 %copy-start.21 = (f32[8]{0:T(128)}, f32[8]{0:T(128)S(1)}, u32[]{:S(2)}) copy-start(f32[8]{0:T(128)S(1)} %get-tuple-element.2092) | copy-start | bytes 100
  110.6 35.7 %copy-start.25 = (f32[8]{0:T(128)}, f32[8]{0:T(128)S(1)}, u32[]{:S(2)}) copy-start(f32[8]{0:T(128)S(1)} %get-tuple-element.2094) | copy-start | bytes 100
  110.6 35.7 %copy-start.27 = (f32[8]{0:T(128)}, f32[8]{0:T(128)S(1)}, u32[]{:S(2)}) copy-start(f32[8]{0:T(128)S(1)} %get-tuple-element.2095) | copy-start | bytes 100
  253.3 36.3 %copy-start.8 = (f32[16,128]{1,0:T(8,128)S(1)}, f32[16,128]{1,0:T(8,128)}, u32[]{:S(2)}) copy-start(f32[16,128]{1,0:T(8,128)} %copy-done.7) | copy-start | bytes 24580
  325.3 40.3 %copy-start.12 = (f32[16,128]{1,0:T(8,128)S(1)}, f32[16,128]{1,0:T(8,128)}, u32[]{:S(2)}) copy-start(f32[16,128]{1,0:T(8,128)} %copy-done.11) | copy-start | bytes 24580
  365.5 39.1 %copy-start.14 = (f32[16,128]{1,0:T(8,128)S(1)}, f32[16,128]{1,0:T(8,128)}, u32[]{:S(2)}) copy-start(f32[16,128]{1,0:T(8,128)} %copy-done.13) | copy-start | bytes 24580
  799.9 149.0 %collective-permute-start.7 = (f32[2,8,16,128]{3,2,1,0:T(8,128)S(1)}, f32[2,8,16,128]{3,2,1,0:T(8,128)S(1)}, u32[]{:S(2)}, u32[]{:S(2)}) collective-permute-start(f32[2,8,16,128]{3,2,1,0:T(8,128)S(1)} %pad_maximum_fusion.4), channel_id=1, source_target_pairs={{0,64},{64,0},{128,192},{192,128},{256,320},{320,256},{384,448},{4... | collective-permute-start | bytes 393224 | tf_op jit(solution)/shard_map/ppermute | solution.py:28
  949.0 6.6 collective-permute-start.8
  955.7 11.0 %collective-permute-start.9 = (f32[2,8,16,128]{3,2,1,0:T(8,128)S(1)}, f32[2,8,16,128]{3,2,1,0:T(8,128)S(1)}, u32[]{:S(2)}, u32[]{:S(2)}) collective-permute-start(f32[2,8,16,128]{3,2,1,0:T(8,128)S(1)} %fusion.50), channel_id=1, source_target_pairs={{0,256},{64,320},{128,384},{192,448},{256,0},{320,64},{384,128},{4... | collective-permute-start | bytes 393224 | tf_op jit(solution)/shard_map/ppermute | solution.py:28
  966.7 13.0 %collective-permute-start.10 = (f32[2,8,16,128]{3,2,1,0:T(8,128)S(1)}, f32[2,8,16,128]{3,2,1,0:T(8,128)S(1)}, u32[]{:S(2)}, u32[]{:S(2)}) collective-permute-start(f32[2,8,16,128]{3,2,1,0:T(8,128)S(1)} %fusion.53), channel_id=1, source_target_pairs={{0,512},{64,576},{128,640},{192,704},{256,768},{320,832},{384,896}... | collective-permute-start | bytes 393224 | tf_op jit(solution)/shard_map/ppermute | solution.py:28
  980.4 3.7 collective-permute-start.11
  980.9 3.2 collective-permute-start.12
  984.2 5.2 collective-permute-start.13
  (143 other events, 339.3 us)
where the time goes:
time: 1010 us; the launch traced here: 990 us
  blocking collectives  440 us (44%)
  starting transfers between devices  199 us (20%)
  other arithmetic  173 us (17%)
  local copies, waits for them, and re-layouts  113 us (11%)
  waiting for transfers between devices  51.9 us (5%)
    all_gather x12, blocking collectives, entering(): pieces = jax.tree.map(lambda part: lax.all_gather(part, axis), value)  440 us
    ppermute x8, starting transfers between devices, from_partner(): lax.ppermute(array, axis, [(i, i ^ 1 << bit) for i in range(lax.axis_size...  177 us
    select_n x189, other arithmetic, hop(): jnp.where(position < mine, new, old)  130 us
    while x252, local copies, waits for them, and re-layouts  81.2 us
    ppermute x8, waiting for transfers between devices, from_partner(): lax.ppermute(array, axis, [(i, i ^ 1 << bit) for i in range(lax.axis_size...  35.9 us
    dynamic_slice x48, local copies, waits for them, and re-layouts, solve_modes(): local_map, _ = lax.scan(compose_row, identity_map, row_inputs_all)  29.9 us
    div x16, other arithmetic, chain_forward(): return tuple((entry / scale_value for entry in entries))  21.4 us
  transfers between devices with their start and end apart: 14, of which 12 were waited for; matrix products, arithmetic and copies ran while one was open for 0% of the time, Pallas kernels for 0%

commit v1 on v0

v1 whole, which is shorter than its diff:
```python
import functools
import math

import jax
import jax.numpy as jnp
import numpy as np
from jax import lax
from jax.experimental import pallas as pl
from jax.experimental.pallas import tpu as pltpu
from jax.sharding import PartitionSpec as P

shift_term = 1.0 / 1024.0
grid_ratio = 1.0 / 128.0
highest = lax.Precision.HIGHEST


def weighted(terms):
    total = None
    for factor, value in terms:
        if abs(factor) < 1e-12:
            continue
        term = value * factor
        total = term if total is None else total + term
    return total


def angle_tables(count):
    half = count // 2
    cosine = [[math.cos(2 * math.pi * (k * i % count) / count) for i in range(count)] for k in range(half + 1)]
    sine = [[math.sin(2 * math.pi * (k * i % count) / count) for i in range(count)] for k in range(half + 1)]
    return cosine, sine


def real_forward(values):
    count = len(values)
    half = count // 2
    cosine, sine = angle_tables(count)
    even = [values[0]] + [values[i] + values[count - i] for i in range(1, half)] + [values[half]]
    odd = [None] + [values[i] - values[count - i] for i in range(1, half)]
    edge, inner = 1 / math.sqrt(count), math.sqrt(2 / count)
    first = weighted([(edge, value) for value in even])
    middle = weighted([(edge * (-1) ** i, value) for i, value in enumerate(even)])
    cosines = [weighted([(inner * cosine[k][i], even[i]) for i in range(half + 1)]) for k in range(1, half)]
    sines = [weighted([(-inner * sine[k][i], odd[i]) for i in range(1, half)]) for k in range(1, half)]
    return [first, middle, *cosines, *sines]


def real_inverse(planes):
    count = len(planes)
    half = count // 2
    cosine, sine = angle_tables(count)
    edge, inner = 1 / math.sqrt(count), math.sqrt(2 / count)
    values = [None] * count
    for i in range(half + 1):
        even = weighted(
            [(edge, planes[0]), (edge * (-1) ** i, planes[1])]
            + [(inner * cosine[k][i], planes[k + 1]) for k in range(1, half)]
        )
        if i in (0, half):
            values[i] = even
            continue
        odd = weighted([(-inner * sine[k][i], planes[half + k]) for k in range(1, half)])
        values[i] = even + odd
        values[count - i] = even - odd
    return values


def plane_modes(count):
    half = count // 2
    return np.array([0, half, *range(1, half), *range(1, half)])


def tables(planes, lanes, blocks, length_x):
    half = blocks // 2
    t = np.arange(lanes)
    phases = np.arange(half)
    turn = 2 * np.pi * phases[:, None] * t[None, :] / length_x
    turns = np.concatenate([np.cos(turn), np.sin(turn)])
    product = 2 * np.pi * (t[:, None] * t[None, :] % lanes) / lanes
    scale = 1 / math.sqrt(lanes)
    c, s = np.cos(product) * scale, np.sin(product) * scale
    inner = np.block([[c, -s], [s, c]])
    root = math.sqrt(2.0)
    n = lanes // 2
    first = np.concatenate([c[:, :1], root * c[:, 1:n], c[:, n : n + 1], -root * s[:, 1:n]], axis=1)
    shifted = np.pi * (t[:, None] * (2 * np.arange(n)[None, :] + 1) % (2 * lanes)) / lanes
    middle = root * scale * np.concatenate([np.cos(shifted), -np.sin(shifted)], axis=1)
    zero = np.zeros((lanes, lanes))
    outer = np.block([[first, zero], [zero, middle]])
    mode_x = np.zeros((half, 2 * lanes))
    mode_x[1:] = phases[1:, None] + blocks * np.concatenate([t, t])[None, :]
    mode_x[0, : n + 1] = blocks * np.arange(n + 1)
    mode_x[0, n + 1 : lanes] = blocks * np.arange(1, n)
    mode_x[0, lanes:] = half + blocks * np.concatenate([np.arange(n), np.arange(n)])
    wave_x = (2 * np.sin(np.pi * mode_x / length_x)) ** 2
    wave_z = (2 * np.sin(np.pi * plane_modes(planes) / planes)) ** 2
    eigen_sum = grid_ratio * grid_ratio * (wave_z[:, None, None] + wave_x[None]) + shift_term
    decay = 2 * np.arcsinh(np.sqrt(eigen_sum) / 2)
    decay = decay.reshape(planes * half, 2 * lanes)
    return tuple(jnp.asarray(a, jnp.float32) for a in (turns, inner, outer, decay))


def places(shape):
    return lax.broadcasted_iota(jnp.int32, shape, 0), lax.broadcasted_iota(jnp.int32, shape, 1)


def column_to_row(column, row, lane):
    return jnp.sum(jnp.where(row == lane, column, 0.0), axis=0, keepdims=True)


def row_to_column(line, row, lane):
    return jnp.sum(jnp.where(row == lane, line, 0.0), axis=1, keepdims=True)


def wall_keep(row, last_row, parts_y):
    is_wall = jnp.logical_and(row == last_row, lax.axis_index("gy") == parts_y - 1)
    return jnp.where(is_wall, 0.0, 1.0)


def source_kernel(planes, parts_y, stream_ref, normal_ref, span_ref, out_ref):
    cells = stream_ref.shape[1]
    rows = stream_ref.shape[0] // planes
    row, lane = places((rows, cells))
    keep = wall_keep(row, rows - 1, parts_y)

    def plane(ref, z):
        return ref[pl.ds(z, rows, stride=planes), :]

    main, rim = [], []
    span_before = plane(span_ref, planes - 1)
    for z in range(planes):
        stream, normal, span = plane(stream_ref, z), plane(normal_ref, z) * keep, plane(span_ref, z)
        stream_left = jnp.where(lane == 0, 0.0, pltpu.roll(stream, 1, 1))
        normal_turned = pltpu.roll(normal, 1, 0)
        normal_below = jnp.where(row == 0, 0.0, normal_turned)
        main.append(
            grid_ratio * (stream - stream_left) + (normal - normal_below) + grid_ratio * (span - span_before)
        )
        ends = column_to_row(stream[:, cells - 1 :], row, lane)
        rim.append(jnp.where(row == 0, -normal_turned, jnp.where(row == 1, -grid_ratio * ends, 0.0)))
        span_before = span
    main, rim = real_forward(main), real_forward(rim)
    for k in range(planes):
        out_ref[k, :rows, :] = main[k]
        out_ref[k, rows:, :] = rim[k]


class Line:
    def __init__(self, decay, rows, parts_y):
        base = (lax.axis_index("gy") * rows).astype(jnp.float32)
        total = rows * parts_y
        self.step = jnp.exp(-decay)
        square, grown = self.step * self.step, jnp.exp(2.0 * decay)
        low = jnp.exp(-decay * (2.0 * base + 1.0))
        high = jnp.exp(-decay * (2.0 * (total - base) - 1.0))
        self.low, self.high = [], []
        for _ in range(rows + 1):
            self.low.append(1.0 + low)
            self.high.append(1.0 + high)
            low, high = low * square, high * grown
        self.decay, self.total = decay, total

    def gain(self):
        return -1.0 / ((jnp.exp(self.decay) - self.step) * (1.0 - jnp.exp(self.decay * (-2.0 * self.total))))


def decay_here(decay_ref, half):
    start = pl.multiple_of(lax.axis_index("gx") * half, half)
    return decay_ref[pl.ds(start, half), :]


def modes_kernel(rows, parts_y, in_ref, turns_ref, inner_ref, outer_ref, decay_ref, send_ref, modes_ref, left, edge):
    blocks, _, lanes = in_ref.shape
    half = blocks // 2
    row, lane = places((rows, lanes))
    main = [in_ref[d, :rows, :] for d in range(blocks)]
    rim = [in_ref[d, rows:, :] for d in range(blocks)]
    for d in range(blocks):
        ends = row_to_column(rim[d - 1][1:2, :], row, lane)
        main[d] = main[d] + jnp.where(lane == 0, ends, 0.0)
    main = real_forward(main)
    rim = real_forward([piece[:1, :] for piece in rim])
    edge[...] = jnp.zeros_like(edge)
    for h in range(2):
        edge[:rows, h * lanes : (h + 1) * lanes] = main[h]
        edge[rows : rows + 1, h * lanes : (h + 1) * lanes] = rim[h]
        left[h, pl.ds(0, rows, stride=half), :] = main[h]
        left[h, rows * half : rows * half + 1, :] = rim[h]
    for a in range(1, half):
        c, s = turns_ref[a : a + 1, :], turns_ref[half + a : half + a + 1, :]
        for first, count, (re, im) in (
            (a, rows, (main[a + 1], main[half + a])),
            (rows * half + a, 1, (rim[a + 1], rim[half + a])),
        ):
            left[0, pl.ds(first, count, stride=half), :] = re * c + im * s
            left[1, pl.ds(first, count, stride=half), :] = im * c - re * s
    inner = jnp.dot(
        jnp.concatenate([left[0], left[1]], axis=1), inner_ref[...], precision=highest, preferred_element_type=jnp.float32
    )
    outer = jnp.dot(edge[...], outer_ref[...], precision=highest, preferred_element_type=jnp.float32)
    for h in range(2):
        part = slice(h * lanes, (h + 1) * lanes)
        modes_ref[h, :, :] = inner[:, part]
        modes_ref[h, pl.ds(0, rows, stride=half), :] = outer[:rows, part]
        modes_ref[h, rows * half : rows * half + 1, :] = outer[rows : rows + 1, part]
    spectrum = row_list(modes_ref, rows, half)
    line = Line(decay_here(decay_ref, half), rows, parts_y)
    below = line.low[0] * spectrum[0]
    above = line.high[rows] * spectrum[rows]
    for i in range(1, rows + 1):
        below = line.low[i] * spectrum[i] + line.step * below
        above = line.high[rows - i] * spectrum[rows - i] + line.step * above
    for copy in range(send_ref.shape[0]):
        send_ref[copy, :half, :] = below
        send_ref[copy, half:, :] = above


def row_list(modes_ref, rows, half):
    return [
        jnp.concatenate([modes_ref[h, i * half : (i + 1) * half, :] for h in range(2)], axis=1)
        for i in range(rows + 1)
    ]


def running(pieces, mine, step, half):
    count = pieces.shape[0]
    below = above = jnp.zeros_like(step)
    below_mine = above_mine = below
    for i in range(count):
        below_mine = jnp.where(mine == i, below, below_mine)
        above_mine = jnp.where(mine == count - 1 - i, above, above_mine)
        below = pieces[i, :half, :] + step * below
        above = pieces[count - 1 - i, half:, :] + step * above
    return below_mine, above_mine, below, above


def near_kernel(rows, near, in_ref, decay_ref, mine_ref, send_ref):
    half = in_ref.shape[1] // 2
    decay = decay_here(decay_ref, half)
    place = lax.rem(lax.axis_index("gy"), near)
    below_mine, above_mine, below, above = running(in_ref, place, jnp.exp(-rows * decay), half)
    mine_ref[:half, :] = below_mine
    mine_ref[half:, :] = above_mine
    for copy in range(send_ref.shape[0]):
        send_ref[copy, :half, :] = below
        send_ref[copy, half:, :] = above


def solve_kernel(
    rows, parts_y, near, in_ref, mine_ref, modes_ref, turns_ref, inner_ref, outer_ref, decay_ref, out_ref, left, edge
):
    blocks, _, lanes = out_ref.shape
    half = blocks // 2
    row, lane = places((rows, lanes))
    decay = decay_here(decay_ref, half)
    place, far_place = lax.rem(lax.axis_index("gy"), near), lax.div(lax.axis_index("gy"), near)
    far_below, far_above, _, _ = running(in_ref, far_place, jnp.exp(-(rows * near) * decay), half)
    ahead = (rows * place).astype(jnp.float32)
    below = mine_ref[:half, :] + jnp.exp(-decay * ahead) * far_below
    above = mine_ref[half:, :] + jnp.exp(-decay * (rows * (near - 1) - ahead)) * far_above
    line = Line(decay, rows, parts_y)
    spectrum = row_list(modes_ref, rows, half)
    gain = line.gain()
    from_below = [line.low[0] * spectrum[0] + below]
    for i in range(1, rows + 1):
        from_below.append(line.low[i] * spectrum[i] + line.step * from_below[-1])
    from_above = above
    edge[...] = jnp.zeros_like(edge)
    for i in reversed(range(rows + 1)):
        solved = gain * (line.high[i] * from_below[i] + line.low[i] * from_above)
        edge[i : i + 1, :] = solved[:1, :]
        for h in range(2):
            left[h, i * half : (i + 1) * half, :] = solved[:, h * lanes : (h + 1) * lanes]
        from_above = line.step * (from_above + line.high[i] * spectrum[i])
    back = (((1,), (1,)), ((), ()))
    inner = lax.dot_general(
        jnp.concatenate([left[0], left[1]], axis=1),
        inner_ref[...],
        back,
        precision=highest,
        preferred_element_type=jnp.float32,
    )
    outer = lax.dot_general(
        edge[...], outer_ref[...], back, precision=highest, preferred_element_type=jnp.float32
    )
    for h in range(2):
        left[h, :, :] = inner[:, h * lanes : (h + 1) * lanes]
    main = [outer[:rows, :lanes], outer[:rows, lanes:]] + [None] * (blocks - 2)
    rim = [outer[rows : rows + 1, :lanes], outer[rows : rows + 1, lanes:]] + [None] * (blocks - 2)
    for a in range(1, half):
        c, s = turns_ref[a : a + 1, :], turns_ref[half + a : half + a + 1, :]
        for planes, first, count in ((main, a, rows), (rim, rows * half + a, 1)):
            re = left[0, pl.ds(first, count, stride=half), :]
            im = left[1, pl.ds(first, count, stride=half), :]
            planes[a + 1] = re * c - im * s
            planes[half + a] = im * c + re * s
    main, rim = real_inverse(main), real_inverse(rim)
    for d in range(blocks):
        out_ref[d, :rows, :] = main[d]
        ends = column_to_row(main[(d + 1) % blocks][:, :1], row, lane)
        out_ref[d, rows:, :] = jnp.where(row == 0, rim[d], jnp.where(row == 1, ends, 0.0))


def correct_kernel(
    parts_y, in_ref, stream_ref, normal_ref, span_ref, pressure_ref, stream_out, normal_out, span_out
):
    planes, _, cells = in_ref.shape
    rows = stream_ref.shape[0] // planes
    row, lane = places((rows, cells))
    keep = wall_keep(row, rows - 1, parts_y)
    pressure = real_inverse([in_ref[k, :rows, :] for k in range(planes)])
    rim = real_inverse([in_ref[k, rows:, :] for k in range(planes)])
    for z in range(planes):
        here = pl.ds(z, rows, stride=planes)
        p = pressure[z]
        upper = jnp.where(row == rows - 1, rim[z][:1, :], pltpu.roll(p, rows - 1, 0))
        right = jnp.where(lane == cells - 1, row_to_column(rim[z][1:2, :], row, lane), pltpu.roll(p, cells - 1, 1))
        pressure_ref[here, :] = p
        stream_out[here, :] = stream_ref[here, :] - grid_ratio * (right - p)
        normal_out[here, :] = (normal_ref[here, :] - (upper - p)) * keep
        span_out[here, :] = span_ref[here, :] - grid_ratio * (pressure[(z + 1) % planes] - p)


def shape_of(*dims):
    return jax.ShapeDtypeStruct(dims, jnp.float32)


def per_device(stream_vel, normal_vel, span_vel):
    rows, planes, cells = stream_vel.shape
    parts_x, parts_y = lax.axis_size("gx"), lax.axis_size("gy")
    blocks, half = parts_x, parts_x // 2
    near = 1 << (parts_y.bit_length() // 2)
    far = parts_y // near
    if planes != parts_x or rows != half or near * far != parts_y:
        raise ValueError("unsupported sizes")
    turns, inner, outer, decay = tables(planes, cells, blocks, cells * parts_x)
    near_groups = [[i * near + k for k in range(near)] for i in range(far)]
    far_groups = [[i + k * near for k in range(far)] for i in range(near)]
    flat = [a.reshape(rows * planes, cells) for a in (stream_vel, normal_vel, span_vel)]
    scratch = [pltpu.VMEM((2, (rows + 1) * half, cells), jnp.float32), pltpu.VMEM((2 * rows, 2 * cells), jnp.float32)]

    sent = pl.pallas_call(
        functools.partial(source_kernel, planes, parts_y), out_shape=shape_of(planes, 2 * rows, cells), name="source"
    )(*flat)
    taken = lax.all_to_all(sent, "gx", 0, 0)
    sent, modes = pl.pallas_call(
        functools.partial(modes_kernel, rows, parts_y),
        out_shape=(shape_of(near, 2 * half, 2 * cells), shape_of(2, (rows + 1) * half, cells)),
        scratch_shapes=scratch,
        name="modes",
    )(taken, turns, inner, outer, decay)
    taken = lax.all_to_all(sent, "gy", 0, 0, axis_index_groups=near_groups)
    mine, sent = pl.pallas_call(
        functools.partial(near_kernel, rows, near),
        out_shape=(shape_of(2 * half, 2 * cells), shape_of(far, 2 * half, 2 * cells)),
        name="near",
    )(taken, decay)
    taken = lax.all_to_all(sent, "gy", 0, 0, axis_index_groups=far_groups)
    sent = pl.pallas_call(
        functools.partial(solve_kernel, rows, parts_y, near),
        out_shape=shape_of(blocks, 2 * rows, cells),
        scratch_shapes=scratch,
        name="solve",
    )(taken, mine, modes, turns, inner, outer, decay)
    taken = lax.all_to_all(sent, "gx", 0, 0)
    outs = pl.pallas_call(
        functools.partial(correct_kernel, parts_y), out_shape=(shape_of(rows * planes, cells),) * 4, name="correct"
    )(taken, *flat)
    return tuple(a.reshape(rows, planes, cells) for a in outs)


def solution(mesh):
    spec = P("gy", None, "gx")
    return jax.shard_map(
        per_device, mesh=mesh, in_specs=(spec,) * 3, out_specs=(spec,) * 4, check_vma=False
    )
```

time: 1010 us -> 85.6 us (0.08); the launches traced: 990 us -> 85 us
  blocking collectives: 440 us -> 74.2 us
  starting transfers between devices: 199 us -> 0 us
  other arithmetic: 173 us -> 0 us
  local copies, waits for them, and re-layouts: 113 us -> 0 us
  waiting for transfers between devices: 51.9 us -> 0 us
  Pallas kernels: 0 us -> 10.2 us
    all_gather x12 -> x0, blocking collectives: 440 us -> none  [entering(): pieces = jax.tree.map(lambda part: lax.all_gather(part, axis), value)]
    ppermute x14 -> x0, starting transfers between devices: 199 us -> none  [the longest x8 177 us: from_partner(): lax.ppermute(array, axis, [(i, i ^ 1 << bit) for i in range(lax.axis_size...]
    select_n x199 -> x0, other arithmetic: 130 us -> none  [the longest x189 130 us: hop(): jnp.where(position < mine, new, old)]
    while x252 -> x0, local copies, waits for them, and re-layouts: 81.2 us -> none
    all_to_all x0 -> x4, blocking collectives: none -> 74.2 us  [the longest x2 42.8 us: per_device(): taken = lax.all_to_all(sent, 'gx', 0, 0)]
    ppermute x14 -> x0, waiting for transfers between devices: 51.9 us -> none  [the longest x8 35.9 us: from_partner(): lax.ppermute(array, axis, [(i, i ^ 1 << bit) for i in range(lax.axis_size...]
    dynamic_slice x48 -> x0, local copies, waits for them, and re-layouts: 29.9 us -> none  [solve_modes(): local_map, _ = lax.scan(compose_row, identity_map, row_inputs_all)]
    div x18 -> x0, other arithmetic: 22.1 us -> none  [the longest x16 21.4 us: chain_forward(): return tuple((entry / scale_value for entry in entries))]
  transfers between devices with their start and end apart: 14 -> 0, of which waited for: 12 -> 0; matrix products, arithmetic and copies ran while one was open for 0% -> 0% of each run, Pallas kernels for 0% -> 0%
where the time goes in v1:
time: 85.6 us; the launch traced here: 85 us
  blocking collectives  74.2 us (87%)
  Pallas kernels  10.2 us (12%)
    all_to_all x2, blocking collectives, per_device(): taken = lax.all_to_all(sent, 'gx', 0, 0)  42.8 us
    all_to_all x1, blocking collectives, per_device(): taken = lax.all_to_all(sent, 'gy', 0, 0, axis_index_groups=far_groups)  17.8 us
    all_to_all x1, blocking collectives, per_device(): taken = lax.all_to_all(sent, 'gy', 0, 0, axis_index_groups=near_groups)  13.6 us
    pallas_call x1, Pallas kernels, per_device(): pl.pallas_call(functools.partial(solve_kernel, rows, parts_y, near), out_...  2.6 us
    pallas_call x1, Pallas kernels, per_device(): pl.pallas_call(functools.partial(modes_kernel, rows, parts_y), out_shape=...  2.31 us
    pallas_call x1, Pallas kernels, per_device(): pl.pallas_call(functools.partial(correct_kernel, parts_y), out_shape=(sha...  1.91 us
    pallas_call x1, Pallas kernels, per_device(): pl.pallas_call(functools.partial(source_kernel, planes, parts_y), out_sha...  1.71 us

profile of v1, /device:TPU:1, one launch (start us, length us, event | category | flops | bytes accessed | tf_op | source)
XLA Modules:
  0.0 85.0 jit_solution(8715593491511750401)
XLA Ops:
  0.6 1.7 %source.1 = f32[16,16,128]{2,1,0:T(8,128)} custom-call(f32[128,128]{1,0:T(8,128)} %bitcast.7, f32[128,128]{1,0:T(8,128)} %bitcast.9, f32[128,128]{1,0:T(8,128)} %bitcast.11), custom_call_target="tpu_custom_call" | custom-call | tf_op jit(solution)/shard_map/source/pallas_call | solution.py:342
  2.3 27.3 %all_to_all.20.in_ref = f32[16,16,128]{2,1,0:T(8,128)} all-to-all(f32[16,16,128]{2,1,0:T(8,128)} %source.1), channel_id=1, replica_groups=mesh['gx'=16,'gy'=64] {'gx'}, dimensions={0} | all-to-all | bytes 262144 | tf_op jit(solution)/shard_map/all_to_all | solution.py:345
  29.7 2.3 %modes.1 = (f32[8,16,256]{2,1,0:T(8,128)}, f32[2,72,128]{2,1,0:T(8,128)}) custom-call(f32[16,16,128]{2,1,0:T(8,128)} %all_to_all.20.in_ref, f32[16,128]{1,0:T(8,128)} %constant.8.clone.turns_ref, f32[256,256]{1,0:T(8,128)} %constant.9.clone.inner_ref, f32[256,256]{1,0:T(8,128)} %constant.10.clone.outer_ref, f32[128,256]{1,0:T(8,128)} %constant.11.clone.decay_ref), custom_call_target="tpu_custom_call" | custom-call | tf_op jit(solution)/shard_map/modes/pallas_call | solution.py:346
  32.0 13.6 %all_to_all.21.in_ref = f32[8,16,256]{2,1,0:T(8,128)} all-to-all(f32[8,16,256]{2,1,0:T(8,128)} %get-tuple-element.12), channel_id=1, replica_groups={{0,1,2,3,4,5,6,7},{8,9,10,11,12,13,14,15},{16,17,18,19,20,21,22,23},{24..., dimensions={0} | all-to-all | bytes 262144 | tf_op jit(solution)/shard_map/all_to_all | solution.py:352
  45.6 1.6 %near.1 = (f32[16,256]{1,0:T(8,128)}, f32[8,16,256]{2,1,0:T(8,128)}) custom-call(f32[8,16,256]{2,1,0:T(8,128)} %all_to_all.21.in_ref, f32[128,256]{1,0:T(8,128)} %constant.11.clone.decay_ref), custom_call_target="tpu_custom_call" | custom-call | tf_op jit(solution)/shard_map/near/pallas_call | solution.py:353
  47.2 17.8 %all_to_all.22.in_ref = f32[8,16,256]{2,1,0:T(8,128)} all-to-all(f32[8,16,256]{2,1,0:T(8,128)} %get-tuple-element.13), channel_id=1, replica_groups={{0,8,16,24,32,40,48,56},{1,9,17,25,33,41,49,57},{2,10,18,26,34,42,50,58..., dimensions={0} | all-to-all | bytes 262144 | tf_op jit(solution)/shard_map/all_to_all | solution.py:358
  65.0 2.6 %solve.1 = f32[16,16,128]{2,1,0:T(8,128)} custom-call(f32[8,16,256]{2,1,0:T(8,128)} %all_to_all.22.in_ref, f32[16,256]{1,0:T(8,128)} %get-tuple-element.14.mine_ref, f32[2,72,128]{2,1,0:T(8,128)} %get-tuple-element.15.modes_ref, f32[16,128]{1,0:T(8,128)} %constant.8.clone.turns_ref, f32[256,256]{1,0:T(8,128)} %constant.9.clone.inner_ref, ...), custom_call_target="tpu_custom_call" | custom-call | tf_op jit(solution)/shard_map/solve/pallas_call | solution.py:359
  67.6 15.5 %all_to_all.23.in_ref = f32[16,16,128]{2,1,0:T(8,128)} all-to-all(f32[16,16,128]{2,1,0:T(8,128)} %solve.1), channel_id=1, replica_groups=mesh['gx'=16,'gy'=64] {'gx'}, dimensions={0} | all-to-all | bytes 262144 | tf_op jit(solution)/shard_map/all_to_all | solution.py:365
  83.1 1.9 %correct.1 = (f32[128,128]{1,0:T(8,128)}, f32[128,128]{1,0:T(8,128)}, f32[128,128]{1,0:T(8,128)}, f32[128,128]{1,0:T(8,128)}) custom-call(f32[16,16,128]{2,1,0:T(8,128)} %all_to_all.23.in_ref, f32[128,128]{1,0:T(8,128)} %bitcast.8, f32[128,128]{1,0:T(8,128)} %bitcast.10, f32[128,128]{1,0:T(8,128)} %bitcast.12), custom_call_target="tpu_custom_call" | custom-call | tf_op jit(solution)/shard_map/correct/pallas_call | solution.py:366

commit v2 on v1

--- a/solution.py
+++ b/solution.py
@@ -210,9 +210,9 @@
     for i in range(1, rows + 1):
         below = line.low[i] * spectrum[i] + line.step * below
         above = line.high[rows - i] * spectrum[rows - i] + line.step * above
-    for copy in range(send_ref.shape[0]):
-        send_ref[copy, :half, :] = below
-        send_ref[copy, half:, :] = above
+    mine = lax.axis_index("gy")
+    for other in range(parts_y):
+        send_ref[other, :, :] = jnp.where(mine < other, below, above)
 
 
 def row_list(modes_ref, rows, half):
@@ -222,42 +222,35 @@
     ]
 
 
-def running(pieces, mine, step, half):
-    count = pieces.shape[0]
-    below = above = jnp.zeros_like(step)
-    below_mine = above_mine = below
-    for i in range(count):
-        below_mine = jnp.where(mine == i, below, below_mine)
-        above_mine = jnp.where(mine == count - 1 - i, above, above_mine)
-        below = pieces[i, :half, :] + step * below
-        above = pieces[count - 1 - i, half:, :] + step * above
-    return below_mine, above_mine, below, above
-
-
-def near_kernel(rows, near, in_ref, decay_ref, mine_ref, send_ref):
-    half = in_ref.shape[1] // 2
-    decay = decay_here(decay_ref, half)
-    place = lax.rem(lax.axis_index("gy"), near)
-    below_mine, above_mine, below, above = running(in_ref, place, jnp.exp(-rows * decay), half)
-    mine_ref[:half, :] = below_mine
-    mine_ref[half:, :] = above_mine
-    for copy in range(send_ref.shape[0]):
-        send_ref[copy, :half, :] = below
-        send_ref[copy, half:, :] = above
+def entering(pieces_ref, mine, step, group):
+    count = pieces_ref.shape[0]
+    zero = jnp.zeros_like(step)
+    below = above = zero
+    for first in range(0, count, group):
+        part = zero
+        kept = jnp.ones_like(step)
+        for i in range(first, min(first + group, count)):
+            part = jnp.where(i < mine, pieces_ref[i] + step * part, part)
+            kept = jnp.where(i < mine, step * kept, kept)
+        below = part + kept * below
+        part = zero
+        kept = jnp.ones_like(step)
+        for i in range(first, min(first + group, count)):
+            j = count - 1 - i
+            part = jnp.where(j > mine, pieces_ref[j] + step * part, part)
+            kept = jnp.where(j > mine, step * kept, kept)
+        above = part + kept * above
+    return below, above
 
 
 def solve_kernel(
-    rows, parts_y, near, in_ref, mine_ref, modes_ref, turns_ref, inner_ref, outer_ref, decay_ref, out_ref, left, edge
+    rows, parts_y, in_ref, modes_ref, turns_ref, inner_ref, outer_ref, decay_ref, out_ref, left, edge
 ):
     blocks, _, lanes = out_ref.shape
     half = blocks // 2
     row, lane = places((rows, lanes))
     decay = decay_here(decay_ref, half)
-    place, far_place = lax.rem(lax.axis_index("gy"), near), lax.div(lax.axis_index("gy"), near)
-    far_below, far_above, _, _ = running(in_ref, far_place, jnp.exp(-(rows * near) * decay), half)
-    ahead = (rows * place).astype(jnp.float32)
-    below = mine_ref[:half, :] + jnp.exp(-decay * ahead) * far_below
-    above = mine_ref[half:, :] + jnp.exp(-decay * (rows * (near - 1) - ahead)) * far_above
+    below, above = entering(in_ref, lax.axis_index("gy"), jnp.exp(-rows * decay), 8)
     line = Line(decay, rows, parts_y)
     spectrum = row_list(modes_ref, rows, half)
     gain = line.gain()
@@ -329,13 +322,9 @@
     rows, planes, cells = stream_vel.shape
     parts_x, parts_y = lax.axis_size("gx"), lax.axis_size("gy")
     blocks, half = parts_x, parts_x // 2
-    near = 1 << (parts_y.bit_length() // 2)
-    far = parts_y // near
-    if planes != parts_x or rows != half or near * far != parts_y:
+    if planes != parts_x or rows != half:
         raise ValueError("unsupported sizes")
     turns, inner, outer, decay = tables(planes, cells, blocks, cells * parts_x)
-    near_groups = [[i * near + k for k in range(near)] for i in range(far)]
-    far_groups = [[i + k * near for k in range(far)] for i in range(near)]
     flat = [a.reshape(rows * planes, cells) for a in (stream_vel, normal_vel, span_vel)]
     scratch = [pltpu.VMEM((2, (rows + 1) * half, cells), jnp.float32), pltpu.VMEM((2 * rows, 2 * cells), jnp.float32)]
 
@@ -345,23 +334,17 @@
     taken = lax.all_to_all(sent, "gx", 0, 0)
     sent, modes = pl.pallas_call(
         functools.partial(modes_kernel, rows, parts_y),
-        out_shape=(shape_of(near, 2 * half, 2 * cells), shape_of(2, (rows + 1) * half, cells)),
+        out_shape=(shape_of(parts_y, half, 2 * cells), shape_of(2, (rows + 1) * half, cells)),
         scratch_shapes=scratch,
         name="modes",
     )(taken, turns, inner, outer, decay)
-    taken = lax.all_to_all(sent, "gy", 0, 0, axis_index_groups=near_groups)
-    mine, sent = pl.pallas_call(
-        functools.partial(near_kernel, rows, near),
-        out_shape=(shape_of(2 * half, 2 * cells), shape_of(far, 2 * half, 2 * cells)),
-        name="near",
-    )(taken, decay)
-    taken = lax.all_to_all(sent, "gy", 0, 0, axis_index_groups=far_groups)
+    taken = lax.all_to_all(sent, "gy", 0, 0)
     sent = pl.pallas_call(
-        functools.partial(solve_kernel, rows, parts_y, near),
+        functools.partial(solve_kernel, rows, parts_y),
         out_shape=shape_of(blocks, 2 * rows, cells),
         scratch_shapes=scratch,
         name="solve",
-    )(taken, mine, modes, turns, inner, outer, decay)
+    )(taken, modes, turns, inner, outer, decay)
     taken = lax.all_to_all(sent, "gx", 0, 0)
     outs = pl.pallas_call(
         functools.partial(correct_kernel, parts_y), out_shape=(shape_of(rows * planes, cells),) * 4, name="correct"

time: 85.6 us -> 83.3 us (0.973)
  Pallas kernels: 10.2 us -> 8.95 us
  blocking collectives: 74.2 us -> 73.3 us
    pallas_call x2 -> x1, Pallas kernels: 4.25 us -> 2.86 us  [per_device(): pl.pallas_call(functools.partial(solve_kernel, rows, parts_y), out_shape=...]
    all_to_all x2, blocking collectives: 42.8 us -> 41.9 us  [per_device(): taken = lax.all_to_all(sent, 'gx', 0, 0)]
    all_to_all x2 -> x1, blocking collectives: 31.4 us -> 31.4 us  [per_device(): taken = lax.all_to_all(sent, 'gy', 0, 0)]
where the time goes in v2:
time: 83.3 us; the launch traced here: 82.9 us
  blocking collectives  73.3 us (88%)
  Pallas kernels  8.95 us (11%)
    all_to_all x2, blocking collectives, per_device(): taken = lax.all_to_all(sent, 'gx', 0, 0)  41.9 us
    all_to_all x1, blocking collectives, per_device(): taken = lax.all_to_all(sent, 'gy', 0, 0)  31.4 us
    pallas_call x1, Pallas kernels, per_device(): pl.pallas_call(functools.partial(solve_kernel, rows, parts_y), out_shape=...  2.86 us
    pallas_call x1, Pallas kernels, per_device(): pl.pallas_call(functools.partial(modes_kernel, rows, parts_y), out_shape=...  2.48 us
    pallas_call x1, Pallas kernels, per_device(): pl.pallas_call(functools.partial(correct_kernel, parts_y), out_shape=(sha...  1.91 us
    pallas_call x1, Pallas kernels, per_device(): pl.pallas_call(functools.partial(source_kernel, planes, parts_y), out_sha...  1.7 us

profile of v2, /device:TPU:1, one launch (start us, length us, event | category | flops | bytes accessed | tf_op | source)
XLA Modules:
  0.0 82.9 jit_solution(12247496316246096368)
XLA Ops:
  0.6 1.7 %source.1 = f32[16,16,128]{2,1,0:T(8,128)} custom-call(f32[128,128]{1,0:T(8,128)} %bitcast.7, f32[128,128]{1,0:T(8,128)} %bitcast.9, f32[128,128]{1,0:T(8,128)} %bitcast.11), custom_call_target="tpu_custom_call" | custom-call | tf_op jit(solution)/shard_map/source/pallas_call | solution.py:331
  2.3 27.3 %all_to_all.15.in_ref = f32[16,16,128]{2,1,0:T(8,128)} all-to-all(f32[16,16,128]{2,1,0:T(8,128)} %source.1), channel_id=1, replica_groups=mesh['gx'=16,'gy'=64] {'gx'}, dimensions={0} | all-to-all | bytes 262144 | tf_op jit(solution)/shard_map/all_to_all | solution.py:334
  29.7 2.5 %modes.1 = (f32[64,8,256]{2,1,0:T(8,128)}, f32[2,72,128]{2,1,0:T(8,128)}) custom-call(f32[16,16,128]{2,1,0:T(8,128)} %all_to_all.15.in_ref, f32[16,128]{1,0:T(8,128)} %constant.8.clone.turns_ref, f32[256,256]{1,0:T(8,128)} %constant.9.clone.inner_ref, f32[256,256]{1,0:T(8,128)} %constant.10.clone.outer_ref, f32[128,256]{1,0:T(8,128)} %constant.11.clone.decay_ref), custom_call_target="tpu_custom_call" | custom-call | tf_op jit(solution)/shard_map/modes/pallas_call | solution.py:335
  32.2 31.4 %all_to_all.16.in_ref = f32[64,8,256]{2,1,0:T(8,128)} all-to-all(f32[64,8,256]{2,1,0:T(8,128)} %get-tuple-element.10), channel_id=1, replica_groups=mesh['gx'=16,'gy'=64] {'gy'}, dimensions={0} | all-to-all | bytes 1048576 | tf_op jit(solution)/shard_map/all_to_all | solution.py:341
  63.6 2.9 %solve.1 = f32[16,16,128]{2,1,0:T(8,128)} custom-call(f32[64,8,256]{2,1,0:T(8,128)} %all_to_all.16.in_ref, f32[2,72,128]{2,1,0:T(8,128)} %get-tuple-element.11.modes_ref, f32[16,128]{1,0:T(8,128)} %constant.8.clone.turns_ref, f32[256,256]{1,0:T(8,128)} %constant.9.clone.inner_ref, f32[256,256]{1,0:T(8,128)} %constant.10.clone.outer_ref, ...), custom_call_target="tpu_custom_call" | custom-call | tf_op jit(solution)/shard_map/solve/pallas_call | solution.py:342
  66.4 14.5 %all_to_all.17.in_ref = f32[16,16,128]{2,1,0:T(8,128)} all-to-all(f32[16,16,128]{2,1,0:T(8,128)} %solve.1), channel_id=1, replica_groups=mesh['gx'=16,'gy'=64] {'gx'}, dimensions={0} | all-to-all | bytes 262144 | tf_op jit(solution)/shard_map/all_to_all | solution.py:348
  81.0 1.9 %correct.1 = (f32[128,128]{1,0:T(8,128)}, f32[128,128]{1,0:T(8,128)}, f32[128,128]{1,0:T(8,128)}, f32[128,128]{1,0:T(8,128)}) custom-call(f32[16,16,128]{2,1,0:T(8,128)} %all_to_all.17.in_ref, f32[128,128]{1,0:T(8,128)} %bitcast.8, f32[128,128]{1,0:T(8,128)} %bitcast.10, f32[128,128]{1,0:T(8,128)} %bitcast.12), custom_call_target="tpu_custom_call" | custom-call | tf_op jit(solution)/shard_map/correct/pallas_call | solution.py:349

commit v3 on v2

--- a/solution.py
+++ b/solution.py
@@ -97,7 +97,26 @@
     eigen_sum = grid_ratio * grid_ratio * (wave_z[:, None, None] + wave_x[None]) + shift_term
     decay = 2 * np.arcsinh(np.sqrt(eigen_sum) / 2)
     decay = decay.reshape(planes * half, 2 * lanes)
-    return tuple(jnp.asarray(a, jnp.float32) for a in (turns, inner, outer, decay))
+    turns = np.concatenate([turns[:half], turns[half:]], axis=1)
+    return jnp.asarray(np.concatenate([inner, outer]), jnp.float32), jnp.asarray(np.concatenate([decay, turns]), jnp.float32)
+
+
+class Tables:
+    def __init__(self, matrix_ref, ref, lanes, half):
+        self.matrix_ref, self.ref, self.lanes, self.half = matrix_ref, ref, lanes, half
+
+    def inner(self):
+        return self.matrix_ref[: 2 * self.lanes, :]
+
+    def outer(self):
+        return self.matrix_ref[2 * self.lanes :, :]
+
+    def decay(self):
+        return self.ref[: self.half, :]
+
+    def turn(self, a):
+        line = self.half + a
+        return self.ref[line : line + 1, : self.lanes], self.ref[line : line + 1, self.lanes :]
 
 
 def places(shape):
@@ -117,7 +136,23 @@
     return jnp.where(is_wall, 0.0, 1.0)
 
 
-def source_kernel(planes, parts_y, stream_ref, normal_ref, span_ref, out_ref):
+def source_kernel(
+    planes, parts_y, stream_hbm, normal_hbm, span_hbm, table_hbm, out_ref, local_ref, stream_ref, normal_ref, span_ref, done
+):
+    half = local_ref.shape[0] // 2
+    decay_rows = pl.ds(pl.multiple_of(lax.axis_index("gx") * half, half), half)
+    turn_rows = pl.ds(table_hbm.shape[0] - half, half)
+    copies = [
+        pltpu.make_async_copy(stream_hbm, stream_ref, done.at[0]),
+        pltpu.make_async_copy(normal_hbm, normal_ref, done.at[1]),
+        pltpu.make_async_copy(span_hbm, span_ref, done.at[2]),
+        pltpu.make_async_copy(table_hbm.at[decay_rows, :], local_ref.at[:half, :], done.at[3]),
+        pltpu.make_async_copy(table_hbm.at[turn_rows, :], local_ref.at[half:, :], done.at[4]),
+    ]
+    for copy in copies:
+        copy.start()
+    for copy in copies[:3]:
+        copy.wait()
     cells = stream_ref.shape[1]
     rows = stream_ref.shape[0] // planes
     row, lane = places((rows, cells))
@@ -143,6 +178,8 @@
     for k in range(planes):
         out_ref[k, :rows, :] = main[k]
         out_ref[k, rows:, :] = rim[k]
+    for copy in copies[3:]:
+        copy.wait()
 
 
 class Line:
@@ -164,14 +201,10 @@
         return -1.0 / ((jnp.exp(self.decay) - self.step) * (1.0 - jnp.exp(self.decay * (-2.0 * self.total))))
 
 
-def decay_here(decay_ref, half):
-    start = pl.multiple_of(lax.axis_index("gx") * half, half)
-    return decay_ref[pl.ds(start, half), :]
-
-
-def modes_kernel(rows, parts_y, in_ref, turns_ref, inner_ref, outer_ref, decay_ref, send_ref, modes_ref, left, edge):
+def modes_kernel(rows, parts_y, in_ref, matrix_ref, table_ref, send_ref, modes_ref, left, edge):
     blocks, _, lanes = in_ref.shape
     half = blocks // 2
+    table = Tables(matrix_ref, table_ref, lanes, half)
     row, lane = places((rows, lanes))
     main = [in_ref[d, :rows, :] for d in range(blocks)]
     rim = [in_ref[d, rows:, :] for d in range(blocks)]
@@ -187,7 +220,7 @@
         left[h, pl.ds(0, rows, stride=half), :] = main[h]
         left[h, rows * half : rows * half + 1, :] = rim[h]
     for a in range(1, half):
-        c, s = turns_ref[a : a + 1, :], turns_ref[half + a : half + a + 1, :]
+        c, s = table.turn(a)
         for first, count, (re, im) in (
             (a, rows, (main[a + 1], main[half + a])),
             (rows * half + a, 1, (rim[a + 1], rim[half + a])),
@@ -195,16 +228,16 @@
             left[0, pl.ds(first, count, stride=half), :] = re * c + im * s
             left[1, pl.ds(first, count, stride=half), :] = im * c - re * s
     inner = jnp.dot(
-        jnp.concatenate([left[0], left[1]], axis=1), inner_ref[...], precision=highest, preferred_element_type=jnp.float32
+        jnp.concatenate([left[0], left[1]], axis=1), table.inner(), precision=highest, preferred_element_type=jnp.float32
     )
-    outer = jnp.dot(edge[...], outer_ref[...], precision=highest, preferred_element_type=jnp.float32)
+    outer = jnp.dot(edge[...], table.outer(), precision=highest, preferred_element_type=jnp.float32)
     for h in range(2):
         part = slice(h * lanes, (h + 1) * lanes)
         modes_ref[h, :, :] = inner[:, part]
         modes_ref[h, pl.ds(0, rows, stride=half), :] = outer[:rows, part]
         modes_ref[h, rows * half : rows * half + 1, :] = outer[rows : rows + 1, part]
     spectrum = row_list(modes_ref, rows, half)
-    line = Line(decay_here(decay_ref, half), rows, parts_y)
+    line = Line(table.decay(), rows, parts_y)
     below = line.low[0] * spectrum[0]
     above = line.high[rows] * spectrum[rows]
     for i in range(1, rows + 1):
@@ -243,13 +276,12 @@
     return below, above
 
 
-def solve_kernel(
-    rows, parts_y, in_ref, modes_ref, turns_ref, inner_ref, outer_ref, decay_ref, out_ref, left, edge
-):
+def solve_kernel(rows, parts_y, in_ref, modes_ref, matrix_ref, table_ref, out_ref, left, edge):
     blocks, _, lanes = out_ref.shape
     half = blocks // 2
+    table = Tables(matrix_ref, table_ref, lanes, half)
     row, lane = places((rows, lanes))
-    decay = decay_here(decay_ref, half)
+    decay = table.decay()
     below, above = entering(in_ref, lax.axis_index("gy"), jnp.exp(-rows * decay), 8)
     line = Line(decay, rows, parts_y)
     spectrum = row_list(modes_ref, rows, half)
@@ -268,20 +300,20 @@
     back = (((1,), (1,)), ((), ()))
     inner = lax.dot_general(
         jnp.concatenate([left[0], left[1]], axis=1),
-        inner_ref[...],
+        table.inner(),
         back,
         precision=highest,
         preferred_element_type=jnp.float32,
     )
     outer = lax.dot_general(
-        edge[...], outer_ref[...], back, precision=highest, preferred_element_type=jnp.float32
+        edge[...], table.outer(), back, precision=highest, preferred_element_type=jnp.float32
     )
     for h in range(2):
         left[h, :, :] = inner[:, h * lanes : (h + 1) * lanes]
     main = [outer[:rows, :lanes], outer[:rows, lanes:]] + [None] * (blocks - 2)
     rim = [outer[rows : rows + 1, :lanes], outer[rows : rows + 1, lanes:]] + [None] * (blocks - 2)
     for a in range(1, half):
-        c, s = turns_ref[a : a + 1, :], turns_ref[half + a : half + a + 1, :]
+        c, s = table.turn(a)
         for planes, first, count in ((main, a, rows), (rim, rows * half + a, 1)):
             re = left[0, pl.ds(first, count, stride=half), :]
             im = left[1, pl.ds(first, count, stride=half), :]
@@ -324,30 +356,41 @@
     blocks, half = parts_x, parts_x // 2
     if planes != parts_x or rows != half:
         raise ValueError("unsupported sizes")
-    turns, inner, outer, decay = tables(planes, cells, blocks, cells * parts_x)
+    matrices, table = tables(planes, cells, blocks, cells * parts_x)
     flat = [a.reshape(rows * planes, cells) for a in (stream_vel, normal_vel, span_vel)]
+    room = pltpu.CompilerParams(vmem_limit_bytes=8 << 20)
     scratch = [pltpu.VMEM((2, (rows + 1) * half, cells), jnp.float32), pltpu.VMEM((2 * rows, 2 * cells), jnp.float32)]
 
-    sent = pl.pallas_call(
-        functools.partial(source_kernel, planes, parts_y), out_shape=shape_of(planes, 2 * rows, cells), name="source"
-    )(*flat)
+    sent, local = pl.pallas_call(
+        functools.partial(source_kernel, planes, parts_y),
+        out_shape=(shape_of(planes, 2 * rows, cells), shape_of(2 * half, 2 * cells)),
+        in_specs=[pl.BlockSpec(memory_space=pltpu.HBM)] * 4,
+        scratch_shapes=[pltpu.VMEM((rows * planes, cells), jnp.float32)] * 3 + [pltpu.SemaphoreType.DMA((5,))],
+        compiler_params=room,
+        name="source",
+    )(*(pltpu.with_memory_space_constraint(a, pltpu.HBM) for a in (*flat, table)))
     taken = lax.all_to_all(sent, "gx", 0, 0)
     sent, modes = pl.pallas_call(
         functools.partial(modes_kernel, rows, parts_y),
         out_shape=(shape_of(parts_y, half, 2 * cells), shape_of(2, (rows + 1) * half, cells)),
         scratch_shapes=scratch,
+        compiler_params=room,
         name="modes",
-    )(taken, turns, inner, outer, decay)
+    )(taken, matrices, local)
     taken = lax.all_to_all(sent, "gy", 0, 0)
     sent = pl.pallas_call(
         functools.partial(solve_kernel, rows, parts_y),
         out_shape=shape_of(blocks, 2 * rows, cells),
         scratch_shapes=scratch,
+        compiler_params=room,
         name="solve",
-    )(taken, modes, turns, inner, outer, decay)
+    )(taken, modes, matrices, local)
     taken = lax.all_to_all(sent, "gx", 0, 0)
     outs = pl.pallas_call(
-        functools.partial(correct_kernel, parts_y), out_shape=(shape_of(rows * planes, cells),) * 4, name="correct"
+        functools.partial(correct_kernel, parts_y),
+        out_shape=(shape_of(rows * planes, cells),) * 4,
+        compiler_params=room,
+        name="correct",
     )(taken, *flat)
     return tuple(a.reshape(rows, planes, cells) for a in outs)
 

time: 83.3 us -> 76.7 us (0.921)
  Pallas kernels: 8.95 us -> 3.64 us
  blocking collectives: 73.3 us -> 72 us
    all_to_all x2, blocking collectives: 41.9 us -> 39.6 us  [per_device(): taken = lax.all_to_all(sent, 'gx', 0, 0)]
    pallas_call x1, Pallas kernels: 2.86 us -> 0.95 us  [per_device(): pl.pallas_call(functools.partial(solve_kernel, rows, parts_y), out_shape=...]
    pallas_call x1, Pallas kernels: 2.48 us -> 0.57 us  [per_device(): pl.pallas_call(functools.partial(modes_kernel, rows, parts_y), out_shape=...]
    all_to_all x1, blocking collectives: 31.4 us -> 32.4 us  [per_device(): taken = lax.all_to_all(sent, 'gy', 0, 0)]
    pallas_call x1, Pallas kernels: 1.91 us -> 0.94 us  [per_device(): pl.pallas_call(functools.partial(correct_kernel, parts_y), out_shape=(sha...]
where the time goes in v3:
time: 76.7 us; the launch traced here: 76.4 us
  blocking collectives  72 us (94%)
  Pallas kernels  3.64 us (5%)
    all_to_all x2, blocking collectives, per_device(): taken = lax.all_to_all(sent, 'gx', 0, 0)  39.6 us
    all_to_all x1, blocking collectives, per_device(): taken = lax.all_to_all(sent, 'gy', 0, 0)  32.4 us

profile of v3, /device:TPU:1, one launch (start us, length us, event | category | flops | bytes accessed | tf_op | source)
XLA Modules:
  0.0 76.4 jit_solution(9683049058128647299)
XLA Ops:
  0.6 0.0 copy-start
  0.6 1.2 %source.1 = (f32[16,16,128]{2,1,0:T(8,128)S(1)}, f32[16,256]{1,0:T(8,128)S(1)}) custom-call(f32[128,128]{1,0:T(8,128)} %bitcast.7, f32[128,128]{1,0:T(8,128)} %bitcast.9, f32[128,128]{1,0:T(8,128)} %bitcast.11, f32[136,256]{1,0:T(8,128)} %constant.5.clone.table_hbm), custom_call_target="tpu_custom_call" | custom-call | tf_op jit(solution)/shard_map/source/pallas_call | solution.py:364
  1.8 25.8 %all_to_all.15.in_ref = f32[16,16,128]{2,1,0:T(8,128)S(1)} all-to-all(f32[16,16,128]{2,1,0:T(8,128)S(1)} %get-tuple-element.12), channel_id=1, replica_groups=mesh['gx'=16,'gy'=64] {'gx'}, dimensions={0} | all-to-all | bytes 262144 | tf_op jit(solution)/shard_map/all_to_all | solution.py:372
  27.6 0.0 copy-done
  27.6 0.6 modes.1
  28.2 32.4 %all_to_all.16.in_ref = f32[64,8,256]{2,1,0:T(8,128)S(1)} all-to-all(f32[64,8,256]{2,1,0:T(8,128)S(1)} %get-tuple-element.14), channel_id=1, replica_groups=mesh['gx'=16,'gy'=64] {'gy'}, dimensions={0} | all-to-all | bytes 1048576 | tf_op jit(solution)/shard_map/all_to_all | solution.py:380
  60.6 0.9 %solve.1 = f32[16,16,128]{2,1,0:T(8,128)S(1)} custom-call(f32[64,8,256]{2,1,0:T(8,128)S(1)} %all_to_all.16.in_ref, f32[2,72,128]{2,1,0:T(8,128)S(1)} %get-tuple-element.15.modes_ref, f32[512,256]{1,0:T(8,128)S(1)} %copy-done, f32[16,256]{1,0:T(8,128)S(1)} %get-tuple-element.13.table_ref), custom_call_target="tpu_custom_call" | custom-call | tf_op jit(solution)/shard_map/solve/pallas_call | solution.py:381
  61.5 0.0 copy-start.1
  61.5 0.0 copy-start.2
  61.6 0.0 copy-start.3
  61.6 13.9 %all_to_all.17.in_ref = f32[16,16,128]{2,1,0:T(8,128)S(1)} all-to-all(f32[16,16,128]{2,1,0:T(8,128)S(1)} %solve.1), channel_id=1, replica_groups=mesh['gx'=16,'gy'=64] {'gx'}, dimensions={0} | all-to-all | bytes 262144 | tf_op jit(solution)/shard_map/all_to_all | solution.py:388
  75.4 0.0 copy-done.1
  75.4 0.0 copy-done.2
  75.4 0.0 copy-done.3
  75.4 0.9 %correct.1 = (f32[128,128]{1,0:T(8,128)}, f32[128,128]{1,0:T(8,128)}, f32[128,128]{1,0:T(8,128)}, f32[128,128]{1,0:T(8,128)}) custom-call(f32[16,16,128]{2,1,0:T(8,128)S(1)} %all_to_all.17.in_ref, f32[128,128]{1,0:T(8,128)S(1)} %bitcast.8, f32[128,128]{1,0:T(8,128)S(1)} %bitcast.10, f32[128,128]{1,0:T(8,128)S(1)} %bitcast.12), custom_call_target="tpu_custom_call" | custom-call | tf_op jit(solution)/shard_map/correct/pallas_call | solution.py:389
Async XLA Ops:
  0.6 27.0 %copy-start = (f32[512,256]{1,0:T(8,128)S(1)}, f32[512,256]{1,0:T(8,128)}, u32[]{:S(2)}) copy-start(f32[512,256]{1,0:T(8,128)} %constant.4.clone.matrix_ref) | copy-start | bytes 1572868
  61.5 13.9 %copy-start.1 = (f32[8,16,128]{2,1,0:T(8,128)S(1)}, f32[8,16,128]{2,1,0:T(8,128)}, u32[]{:S(2)}) copy-start(f32[8,16,128]{2,1,0:T(8,128)} %param.5) | copy-start | bytes 196612
  61.5 13.9 %copy-start.2 = (f32[8,16,128]{2,1,0:T(8,128)S(1)}, f32[8,16,128]{2,1,0:T(8,128)}, u32[]{:S(2)}) copy-start(f32[8,16,128]{2,1,0:T(8,128)} %param.6) | copy-start | bytes 196612
  61.6 13.9 %copy-start.3 = (f32[8,16,128]{2,1,0:T(8,128)S(1)}, f32[8,16,128]{2,1,0:T(8,128)}, u32[]{:S(2)}) copy-start(f32[8,16,128]{2,1,0:T(8,128)} %param.7) | copy-start | bytes 196612

commit v4 on v3

--- a/solution.py
+++ b/solution.py
@@ -243,9 +243,9 @@
     for i in range(1, rows + 1):
         below = line.low[i] * spectrum[i] + line.step * below
         above = line.high[rows - i] * spectrum[rows - i] + line.step * above
-    mine = lax.axis_index("gy")
-    for other in range(parts_y):
-        send_ref[other, :, :] = jnp.where(mine < other, below, above)
+    for other in range(send_ref.shape[0]):
+        send_ref[other, :half, :] = below
+        send_ref[other, half:, :] = above
 
 
 def row_list(modes_ref, rows, half):
@@ -255,34 +255,42 @@
     ]
 
 
-def entering(pieces_ref, mine, step, group):
+def near_kernel(rows, near, in_ref, table_ref, mine_ref, send_ref):
+    half = in_ref.shape[1] // 2
+    step = jnp.exp(-rows * table_ref[:half, :])
+    place, group = lax.rem(lax.axis_index("gy"), near), lax.div(lax.axis_index("gy"), near)
+    below = above = jnp.zeros_like(step)
+    for i in range(near):
+        j = near - 1 - i
+        mine_ref[:half, :] = jnp.where(place == i, below, mine_ref[:half, :]) if i else below
+        mine_ref[half:, :] = jnp.where(place == j, above, mine_ref[half:, :]) if i else above
+        below = in_ref[i, :half, :] + step * below
+        above = in_ref[j, half:, :] + step * above
+    for other in range(send_ref.shape[0]):
+        send_ref[other, :, :] = jnp.where(group < other, below, above)
+
+
+def entering(pieces_ref, mine, step):
     count = pieces_ref.shape[0]
-    zero = jnp.zeros_like(step)
-    below = above = zero
-    for first in range(0, count, group):
-        part = zero
-        kept = jnp.ones_like(step)
-        for i in range(first, min(first + group, count)):
-            part = jnp.where(i < mine, pieces_ref[i] + step * part, part)
-            kept = jnp.where(i < mine, step * kept, kept)
-        below = part + kept * below
-        part = zero
-        kept = jnp.ones_like(step)
-        for i in range(first, min(first + group, count)):
-            j = count - 1 - i
-            part = jnp.where(j > mine, pieces_ref[j] + step * part, part)
-            kept = jnp.where(j > mine, step * kept, kept)
-        above = part + kept * above
+    below = above = jnp.zeros_like(step)
+    for i in range(count):
+        j = count - 1 - i
+        below = jnp.where(i < mine, pieces_ref[i] + step * below, below)
+        above = jnp.where(j > mine, pieces_ref[j] + step * above, above)
     return below, above
 
 
-def solve_kernel(rows, parts_y, in_ref, modes_ref, matrix_ref, table_ref, out_ref, left, edge):
+def solve_kernel(rows, parts_y, near, in_ref, mine_ref, modes_ref, matrix_ref, table_ref, out_ref, left, edge):
     blocks, _, lanes = out_ref.shape
     half = blocks // 2
     table = Tables(matrix_ref, table_ref, lanes, half)
     row, lane = places((rows, lanes))
     decay = table.decay()
-    below, above = entering(in_ref, lax.axis_index("gy"), jnp.exp(-rows * decay), 8)
+    place, group = lax.rem(lax.axis_index("gy"), near), lax.div(lax.axis_index("gy"), near)
+    far_below, far_above = entering(in_ref, group, jnp.exp(-(rows * near) * decay))
+    ahead = (rows * place).astype(jnp.float32)
+    below = mine_ref[:half, :] + jnp.exp(-decay * ahead) * far_below
+    above = mine_ref[half:, :] + jnp.exp(-decay * (rows * (near - 1) - ahead)) * far_above
     line = Line(decay, rows, parts_y)
     spectrum = row_list(modes_ref, rows, half)
     gain = line.gain()
@@ -354,9 +362,13 @@
     rows, planes, cells = stream_vel.shape
     parts_x, parts_y = lax.axis_size("gx"), lax.axis_size("gy")
     blocks, half = parts_x, parts_x // 2
-    if planes != parts_x or rows != half:
+    near = 1 << (parts_y.bit_length() // 2)
+    far = parts_y // near
+    if planes != parts_x or rows != half or near * far != parts_y:
         raise ValueError("unsupported sizes")
     matrices, table = tables(planes, cells, blocks, cells * parts_x)
+    near_groups = [[i * near + k for k in range(near)] for i in range(far)]
+    far_groups = [[i + k * near for k in range(far)] for i in range(near)]
     flat = [a.reshape(rows * planes, cells) for a in (stream_vel, normal_vel, span_vel)]
     room = pltpu.CompilerParams(vmem_limit_bytes=8 << 20)
     scratch = [pltpu.VMEM((2, (rows + 1) * half, cells), jnp.float32), pltpu.VMEM((2 * rows, 2 * cells), jnp.float32)]
@@ -372,19 +384,26 @@
     taken = lax.all_to_all(sent, "gx", 0, 0)
     sent, modes = pl.pallas_call(
         functools.partial(modes_kernel, rows, parts_y),
-        out_shape=(shape_of(parts_y, half, 2 * cells), shape_of(2, (rows + 1) * half, cells)),
+        out_shape=(shape_of(near, 2 * half, 2 * cells), shape_of(2, (rows + 1) * half, cells)),
         scratch_shapes=scratch,
         compiler_params=room,
         name="modes",
     )(taken, matrices, local)
-    taken = lax.all_to_all(sent, "gy", 0, 0)
+    taken = lax.all_to_all(sent, "gy", 0, 0, axis_index_groups=near_groups)
+    mine, sent = pl.pallas_call(
+        functools.partial(near_kernel, rows, near),
+        out_shape=(shape_of(2 * half, 2 * cells), shape_of(far, half, 2 * cells)),
+        compiler_params=room,
+        name="near",
+    )(taken, local)
+    taken = lax.all_to_all(sent, "gy", 0, 0, axis_index_groups=far_groups)
     sent = pl.pallas_call(
-        functools.partial(solve_kernel, rows, parts_y),
+        functools.partial(solve_kernel, rows, parts_y, near),
         out_shape=shape_of(blocks, 2 * rows, cells),
         scratch_shapes=scratch,
         compiler_params=room,
         name="solve",
-    )(taken, modes, matrices, local)
+    )(taken, mine, modes, matrices, local)
     taken = lax.all_to_all(sent, "gx", 0, 0)
     outs = pl.pallas_call(
         functools.partial(correct_kernel, parts_y),

time: 76.7 us -> 75.4 us (0.983)
  blocking collectives: 72 us -> 70.9 us
    all_to_all x1 -> x2, blocking collectives: 32.4 us -> 31.6 us  [the longest x1 19.6 us: per_device(): taken = lax.all_to_all(sent, 'gy', 0, 0, axis_index_groups=far_groups)]
where the time goes in v4:
time: 75.4 us; the launch traced here: 75.1 us
  blocking collectives  70.9 us (94%)
  Pallas kernels  3.43 us (5%)
    all_to_all x2, blocking collectives, per_device(): taken = lax.all_to_all(sent, 'gx', 0, 0)  39.4 us
    all_to_all x1, blocking collectives, per_device(): taken = lax.all_to_all(sent, 'gy', 0, 0, axis_index_groups=far_groups)  19.6 us
    all_to_all x1, blocking collectives, per_device(): taken = lax.all_to_all(sent, 'gy', 0, 0, axis_index_groups=near_groups)  12 us

profile of v4, /device:TPU:1, one launch (start us, length us, event | category | flops | bytes accessed | tf_op | source)
XLA Modules:
  0.0 75.1 jit_solution(456785901847329778)
XLA Ops:
  0.6 0.0 copy-start
  0.6 1.2 %source.1 = (f32[16,16,128]{2,1,0:T(8,128)S(1)}, f32[16,256]{1,0:T(8,128)S(1)}) custom-call(f32[128,128]{1,0:T(8,128)} %bitcast.7, f32[128,128]{1,0:T(8,128)} %bitcast.9, f32[128,128]{1,0:T(8,128)} %bitcast.11, f32[136,256]{1,0:T(8,128)} %constant.5.clone.table_hbm), custom_call_target="tpu_custom_call" | custom-call | tf_op jit(solution)/shard_map/source/pallas_call | solution.py:376
  1.8 25.8 %all_to_all.20.in_ref = f32[16,16,128]{2,1,0:T(8,128)S(1)} all-to-all(f32[16,16,128]{2,1,0:T(8,128)S(1)} %get-tuple-element.14), channel_id=1, replica_groups=mesh['gx'=16,'gy'=64] {'gx'}, dimensions={0} | all-to-all | bytes 262144 | tf_op jit(solution)/shard_map/all_to_all | solution.py:384
  27.6 0.0 copy-done
  27.6 0.5 modes.1
  28.1 12.0 %all_to_all.21.in_ref = f32[8,16,256]{2,1,0:T(8,128)S(1)} all-to-all(f32[8,16,256]{2,1,0:T(8,128)S(1)} %get-tuple-element.16), channel_id=1, replica_groups={{0,1,2,3,4,5,6,7},{8,9,10,11,12,13,14,15},{16,17,18,19,20,21,22,23},{24..., dimensions={0} | all-to-all | bytes 262144 | tf_op jit(solution)/shard_map/all_to_all | solution.py:392
  40.2 19.6 %all_to_all.22.in_ref = f32[8,8,256]{2,1,0:T(8,128)S(1)} all-to-all(f32[8,8,256]{2,1,0:T(8,128)S(1)} %get-tuple-element.17), channel_id=1, replica_groups={{0,8,16,24,32,40,48,56},{1,9,17,25,33,41,49,57},{2,10,18,26,34,42,50,58..., dimensions={0} | all-to-all | bytes 131072 | tf_op jit(solution)/shard_map/all_to_all | solution.py:399
  59.7 0.8 %solve.1 = f32[16,16,128]{2,1,0:T(8,128)S(1)} custom-call(f32[8,8,256]{2,1,0:T(8,128)S(1)} %all_to_all.22.in_ref, f32[16,256]{1,0:T(8,128)S(1)} %get-tuple-element.18.mine_ref, f32[2,72,128]{2,1,0:T(8,128)S(1)} %get-tuple-element.19.modes_ref, f32[512,256]{1,0:T(8,128)S(1)} %copy-done, f32[16,256]{1,0:T(8,128)S(1)} %get-tuple-element.15.table_ref), custom_call_target="tpu_custom_call" | custom-call | tf_op jit(solution)/shard_map/solve/pallas_call | solution.py:400
  60.5 0.0 copy-start.1
  60.5 0.0 copy-start.2
  60.5 0.0 copy-start.3
  60.5 13.6 %all_to_all.23.in_ref = f32[16,16,128]{2,1,0:T(8,128)S(1)} all-to-all(f32[16,16,128]{2,1,0:T(8,128)S(1)} %solve.1), channel_id=1, replica_groups=mesh['gx'=16,'gy'=64] {'gx'}, dimensions={0} | all-to-all | bytes 262144 | tf_op jit(solution)/shard_map/all_to_all | solution.py:407
  74.1 0.0 copy-done.1
  74.1 0.0 copy-done.2
  74.1 0.0 copy-done.3
  74.2 0.9 %correct.1 = (f32[128,128]{1,0:T(8,128)}, f32[128,128]{1,0:T(8,128)}, f32[128,128]{1,0:T(8,128)}, f32[128,128]{1,0:T(8,128)}) custom-call(f32[16,16,128]{2,1,0:T(8,128)S(1)} %all_to_all.23.in_ref, f32[128,128]{1,0:T(8,128)S(1)} %bitcast.8, f32[128,128]{1,0:T(8,128)S(1)} %bitcast.10, f32[128,128]{1,0:T(8,128)S(1)} %bitcast.12), custom_call_target="tpu_custom_call" | custom-call | tf_op jit(solution)/shard_map/correct/pallas_call | solution.py:408
  (1 shorter events, 0.0 us)
Async XLA Ops:
  0.6 27.0 %copy-start = (f32[512,256]{1,0:T(8,128)S(1)}, f32[512,256]{1,0:T(8,128)}, u32[]{:S(2)}) copy-start(f32[512,256]{1,0:T(8,128)} %constant.4.clone.matrix_ref) | copy-start | bytes 1572868
  60.5 13.6 %copy-start.1 = (f32[8,16,128]{2,1,0:T(8,128)S(1)}, f32[8,16,128]{2,1,0:T(8,128)}, u32[]{:S(2)}) copy-start(f32[8,16,128]{2,1,0:T(8,128)} %param.5) | copy-start | bytes 196612
  60.5 13.6 %copy-start.2 = (f32[8,16,128]{2,1,0:T(8,128)S(1)}, f32[8,16,128]{2,1,0:T(8,128)}, u32[]{:S(2)}) copy-start(f32[8,16,128]{2,1,0:T(8,128)} %param.6) | copy-start | bytes 196612
  60.5 13.6 %copy-start.3 = (f32[8,16,128]{2,1,0:T(8,128)S(1)}, f32[8,16,128]{2,1,0:T(8,128)}, u32[]{:S(2)}) copy-start(f32[8,16,128]{2,1,0:T(8,128)} %param.7) | copy-start | bytes 196612

commit v5 on v4

--- a/solution.py
+++ b/solution.py
@@ -137,7 +137,20 @@
 
 
 def source_kernel(
-    planes, parts_y, stream_hbm, normal_hbm, span_hbm, table_hbm, out_ref, local_ref, stream_ref, normal_ref, span_ref, done
+    planes,
+    parts_y,
+    stream_hbm,
+    normal_hbm,
+    span_hbm,
+    table_hbm,
+    matrix_hbm,
+    out_ref,
+    local_ref,
+    matrix_ref,
+    stream_ref,
+    normal_ref,
+    span_ref,
+    done,
 ):
     half = local_ref.shape[0] // 2
     decay_rows = pl.ds(pl.multiple_of(lax.axis_index("gx") * half, half), half)
@@ -148,6 +161,7 @@
         pltpu.make_async_copy(span_hbm, span_ref, done.at[2]),
         pltpu.make_async_copy(table_hbm.at[decay_rows, :], local_ref.at[:half, :], done.at[3]),
         pltpu.make_async_copy(table_hbm.at[turn_rows, :], local_ref.at[half:, :], done.at[4]),
+        pltpu.make_async_copy(matrix_hbm, matrix_ref, done.at[5]),
     ]
     for copy in copies:
         copy.start()
@@ -176,10 +190,24 @@
         span_before = span
     main, rim = real_forward(main), real_forward(rim)
     for k in range(planes):
-        out_ref[k, :rows, :] = main[k]
-        out_ref[k, rows:, :] = rim[k]
+        put(out_ref, k, main[k], rim[k])
     for copy in copies[3:]:
         copy.wait()
+
+
+def put(ref, index, main, rim):
+    pairs = ref.shape[1] - 1
+    for j in range(pairs):
+        ref[index, j] = main[2 * j : 2 * j + 2, :]
+    ref[index, pairs] = rim[:2, :]
+
+
+def take(ref, held):
+    count, pairs = ref.shape[0], ref.shape[1] - 1
+    for i in range(count):
+        for j in range(pairs):
+            held[i, 2 * j : 2 * j + 2, :] = ref[i, j]
+    return [held[i] for i in range(count)], [ref[i, pairs] for i in range(count)]
 
 
 class Line:
@@ -201,13 +229,12 @@
         return -1.0 / ((jnp.exp(self.decay) - self.step) * (1.0 - jnp.exp(self.decay * (-2.0 * self.total))))
 
 
-def modes_kernel(rows, parts_y, in_ref, matrix_ref, table_ref, send_ref, modes_ref, left, edge):
-    blocks, _, lanes = in_ref.shape
+def modes_kernel(rows, parts_y, in_ref, matrix_ref, table_ref, send_ref, modes_ref, left, edge, held):
+    blocks, _, _, lanes = in_ref.shape
     half = blocks // 2
     table = Tables(matrix_ref, table_ref, lanes, half)
     row, lane = places((rows, lanes))
-    main = [in_ref[d, :rows, :] for d in range(blocks)]
-    rim = [in_ref[d, rows:, :] for d in range(blocks)]
+    main, rim = take(in_ref, held)
     for d in range(blocks):
         ends = row_to_column(rim[d - 1][1:2, :], row, lane)
         main[d] = main[d] + jnp.where(lane == 0, ends, 0.0)
@@ -281,7 +308,7 @@
 
 
 def solve_kernel(rows, parts_y, near, in_ref, mine_ref, modes_ref, matrix_ref, table_ref, out_ref, left, edge):
-    blocks, _, lanes = out_ref.shape
+    blocks, _, _, lanes = out_ref.shape
     half = blocks // 2
     table = Tables(matrix_ref, table_ref, lanes, half)
     row, lane = places((rows, lanes))
@@ -329,20 +356,19 @@
             planes[half + a] = im * c + re * s
     main, rim = real_inverse(main), real_inverse(rim)
     for d in range(blocks):
-        out_ref[d, :rows, :] = main[d]
         ends = column_to_row(main[(d + 1) % blocks][:, :1], row, lane)
-        out_ref[d, rows:, :] = jnp.where(row == 0, rim[d], jnp.where(row == 1, ends, 0.0))
+        put(out_ref, d, main[d], jnp.where(row == 0, rim[d], ends))
 
 
 def correct_kernel(
-    parts_y, in_ref, stream_ref, normal_ref, span_ref, pressure_ref, stream_out, normal_out, span_out
+    parts_y, in_ref, stream_ref, normal_ref, span_ref, pressure_ref, stream_out, normal_out, span_out, held
 ):
-    planes, _, cells = in_ref.shape
+    planes, _, _, cells = in_ref.shape
     rows = stream_ref.shape[0] // planes
     row, lane = places((rows, cells))
     keep = wall_keep(row, rows - 1, parts_y)
-    pressure = real_inverse([in_ref[k, :rows, :] for k in range(planes)])
-    rim = real_inverse([in_ref[k, rows:, :] for k in range(planes)])
+    pressure, rim = take(in_ref, held)
+    pressure, rim = real_inverse(pressure), real_inverse(rim)
     for z in range(planes):
         here = pl.ds(z, rows, stride=planes)
         p = pressure[z]
@@ -370,22 +396,26 @@
     near_groups = [[i * near + k for k in range(near)] for i in range(far)]
     far_groups = [[i + k * near for k in range(far)] for i in range(near)]
     flat = [a.reshape(rows * planes, cells) for a in (stream_vel, normal_vel, span_vel)]
+    message = shape_of(blocks, rows // 2 + 1, 2, cells)
+    held = pltpu.VMEM((blocks, rows, cells), jnp.float32)
     room = pltpu.CompilerParams(vmem_limit_bytes=8 << 20)
     scratch = [pltpu.VMEM((2, (rows + 1) * half, cells), jnp.float32), pltpu.VMEM((2 * rows, 2 * cells), jnp.float32)]
 
-    sent, local = pl.pallas_call(
+    kept = [matrices, *flat]
+    sent, local, *kept = pl.pallas_call(
         functools.partial(source_kernel, planes, parts_y),
-        out_shape=(shape_of(planes, 2 * rows, cells), shape_of(2 * half, 2 * cells)),
-        in_specs=[pl.BlockSpec(memory_space=pltpu.HBM)] * 4,
-        scratch_shapes=[pltpu.VMEM((rows * planes, cells), jnp.float32)] * 3 + [pltpu.SemaphoreType.DMA((5,))],
+        out_shape=(message, shape_of(2 * half, 2 * cells), *(shape_of(*a.shape) for a in kept)),
+        in_specs=[pl.BlockSpec(memory_space=pltpu.HBM)] * 5,
+        scratch_shapes=[pltpu.SemaphoreType.DMA((6,))],
         compiler_params=room,
         name="source",
-    )(*(pltpu.with_memory_space_constraint(a, pltpu.HBM) for a in (*flat, table)))
+    )(*(pltpu.with_memory_space_constraint(a, pltpu.HBM) for a in (*flat, table, matrices)))
+    matrices, *flat = kept
     taken = lax.all_to_all(sent, "gx", 0, 0)
     sent, modes = pl.pallas_call(
         functools.partial(modes_kernel, rows, parts_y),
         out_shape=(shape_of(near, 2 * half, 2 * cells), shape_of(2, (rows + 1) * half, cells)),
-        scratch_shapes=scratch,
+        scratch_shapes=[*scratch, held],
         compiler_params=room,
         name="modes",
     )(taken, matrices, local)
@@ -399,7 +429,7 @@
     taken = lax.all_to_all(sent, "gy", 0, 0, axis_index_groups=far_groups)
     sent = pl.pallas_call(
         functools.partial(solve_kernel, rows, parts_y, near),
-        out_shape=shape_of(blocks, 2 * rows, cells),
+        out_shape=message,
         scratch_shapes=scratch,
         compiler_params=room,
         name="solve",
@@ -408,6 +438,7 @@
     outs = pl.pallas_call(
         functools.partial(correct_kernel, parts_y),
         out_shape=(shape_of(rows * planes, cells),) * 4,
+        scratch_shapes=[held],
         compiler_params=room,
         name="correct",
     )(taken, *flat)

time: 75.4 us -> 73.2 us (0.971)
  blocking collectives: 70.9 us -> 68.8 us
    all_to_all x2, blocking collectives: 39.4 us -> 38.2 us  [per_device(): taken = lax.all_to_all(sent, 'gx', 0, 0)]
    all_to_all x1, blocking collectives: 19.6 us -> 18.8 us  [per_device(): taken = lax.all_to_all(sent, 'gy', 0, 0, axis_index_groups=far_groups)]
where the time goes in v5:
time: 73.2 us; the launch traced here: 72.9 us
  blocking collectives  68.8 us (94%)
  Pallas kernels  3.49 us (5%)
    all_to_all x2, blocking collectives, per_device(): taken = lax.all_to_all(sent, 'gx', 0, 0)  38.2 us
    all_to_all x1, blocking collectives, per_device(): taken = lax.all_to_all(sent, 'gy', 0, 0, axis_index_groups=far_groups)  18.8 us
    all_to_all x1, blocking collectives, per_device(): taken = lax.all_to_all(sent, 'gy', 0, 0, axis_index_groups=near_groups)  11.8 us

profile of v5, /device:TPU:1, one launch (start us, length us, event | category | flops | bytes accessed | tf_op | source)
XLA Modules:
  0.0 72.9 jit_solution(8694054580102123038)
XLA Ops:
  0.6 1.2 %source.1 = (f32[16,5,2,128]{3,2,1,0:T(2,128)S(1)}, f32[16,256]{1,0:T(8,128)S(1)}, f32[512,256]{1,0:T(8,128)S(1)}, f32[128,128]{1,0:T(8,128)S(1)}, f32[128,128]{1,0:T(8,128)S(1)}, /*index=5*/f32[128,128]{1,0:T(8,128)S(1)}) custom-call(f32[128,128]{1,0:T(8,128)} %bitcast.7, f32[128,128]{1,0:T(8,128)} %bitcast.8, f32[128,128]{1,0:T(8,128)} %bitcast.9, ...), custom_call_target="tpu_custom_call" | custom-call | tf_op jit(solution)/shard_map/source/pallas_call | solution.py:405
  1.9 24.7 %all_to_all.20.in_ref = f32[16,5,2,128]{3,2,1,0:T(2,128)S(1)} all-to-all(f32[16,5,2,128]{3,2,1,0:T(2,128)S(1)} %get-tuple-element.18), channel_id=1, replica_groups=mesh['gx'=16,'gy'=64] {'gx'}, dimensions={0} | all-to-all | bytes 163840 | tf_op jit(solution)/shard_map/all_to_all | solution.py:414
  26.6 0.5 modes.1
  27.1 11.8 %all_to_all.21.in_ref = f32[8,16,256]{2,1,0:T(8,128)S(1)} all-to-all(f32[8,16,256]{2,1,0:T(8,128)S(1)} %get-tuple-element.21), channel_id=1, replica_groups={{0,1,2,3,4,5,6,7},{8,9,10,11,12,13,14,15},{16,17,18,19,20,21,22,23},{24..., dimensions={0} | all-to-all | bytes 262144 | tf_op jit(solution)/shard_map/all_to_all | solution.py:422
  39.0 18.8 %all_to_all.22.in_ref = f32[8,8,256]{2,1,0:T(8,128)S(1)} all-to-all(f32[8,8,256]{2,1,0:T(8,128)S(1)} %get-tuple-element.22), channel_id=1, replica_groups={{0,8,16,24,32,40,48,56},{1,9,17,25,33,41,49,57},{2,10,18,26,34,42,50,58..., dimensions={0} | all-to-all | bytes 131072 | tf_op jit(solution)/shard_map/all_to_all | solution.py:429
  57.7 0.8 %solve.1 = f32[16,5,2,128]{3,2,1,0:T(2,128)S(1)} custom-call(f32[8,8,256]{2,1,0:T(8,128)S(1)} %all_to_all.22.in_ref, f32[16,256]{1,0:T(8,128)S(1)} %get-tuple-element.23.mine_ref, f32[2,72,128]{2,1,0:T(8,128)S(1)} %get-tuple-element.24.modes_ref, f32[512,256]{1,0:T(8,128)S(1)} %get-tuple-element.19.matrix_ref, f32[16,256]{1,0:T(8,128)S(1)} %get-tuple-element.20.table_ref), custom_call_target="tpu_custom_call" | custom-call | tf_op jit(solution)/shard_map/solve/pallas_call | solution.py:430
  58.5 13.4 %all_to_all.23.in_ref = f32[16,5,2,128]{3,2,1,0:T(2,128)S(1)} all-to-all(f32[16,5,2,128]{3,2,1,0:T(2,128)S(1)} %solve.1), channel_id=1, replica_groups=mesh['gx'=16,'gy'=64] {'gx'}, dimensions={0} | all-to-all | bytes 163840 | tf_op jit(solution)/shard_map/all_to_all | solution.py:437
  72.0 0.9 %correct.1 = (f32[128,128]{1,0:T(8,128)}, f32[128,128]{1,0:T(8,128)}, f32[128,128]{1,0:T(8,128)}, f32[128,128]{1,0:T(8,128)}) custom-call(f32[16,5,2,128]{3,2,1,0:T(2,128)S(1)} %all_to_all.23.in_ref, f32[128,128]{1,0:T(8,128)S(1)} %get-tuple-element.25.stream_ref, f32[128,128]{1,0:T(8,128)S(1)} %get-tuple-element.26.normal_ref, ...), custom_call_target="tpu_custom_call" | custom-call | tf_op jit(solution)/shard_map/correct/pallas_call | solution.py:438
  (1 shorter events, 0.0 us)

commit v6 on v5

--- a/solution.py
+++ b/solution.py
@@ -3,6 +3,7 @@
 
 import jax
 import jax.numpy as jnp
+import ml_dtypes
 import numpy as np
 from jax import lax
 from jax.experimental import pallas as pl
@@ -11,7 +12,6 @@
 
 shift_term = 1.0 / 1024.0
 grid_ratio = 1.0 / 128.0
-highest = lax.Precision.HIGHEST
 
 
 def weighted(terms):
@@ -85,8 +85,7 @@
     first = np.concatenate([c[:, :1], root * c[:, 1:n], c[:, n : n + 1], -root * s[:, 1:n]], axis=1)
     shifted = np.pi * (t[:, None] * (2 * np.arange(n)[None, :] + 1) % (2 * lanes)) / lanes
     middle = root * scale * np.concatenate([np.cos(shifted), -np.sin(shifted)], axis=1)
-    zero = np.zeros((lanes, lanes))
-    outer = np.block([[first, zero], [zero, middle]])
+    outer = np.concatenate([first, middle], axis=1)
     mode_x = np.zeros((half, 2 * lanes))
     mode_x[1:] = phases[1:, None] + blocks * np.concatenate([t, t])[None, :]
     mode_x[0, : n + 1] = blocks * np.arange(n + 1)
@@ -98,18 +97,49 @@
     decay = 2 * np.arcsinh(np.sqrt(eigen_sum) / 2)
     decay = decay.reshape(planes * half, 2 * lanes)
     turns = np.concatenate([turns[:half], turns[half:]], axis=1)
-    return jnp.asarray(np.concatenate([inner, outer]), jnp.float32), jnp.asarray(np.concatenate([decay, turns]), jnp.float32)
+    matrices = np.concatenate([inner, outer])
+    parts = []
+    for _ in range(3):
+        parts.append(matrices.astype(ml_dtypes.bfloat16))
+        matrices = matrices - parts[-1].astype(np.float64)
+    return jnp.asarray(np.concatenate(parts)), jnp.asarray(np.concatenate([decay, turns]), jnp.float32)
+
+
+def split(values, count):
+    parts = []
+    for _ in range(count):
+        parts.append(values.astype(jnp.bfloat16))
+        values = values - parts[-1].astype(jnp.float32)
+    return parts
+
+
+def product(values, matrix, transposed=False):
+    parts, rows = split(values, len(matrix)), values.shape[0]
+    dims = (((1,), (1 if transposed else 0,)), ((), ()))
+    terms = []
+    for j, piece in enumerate(matrix):
+        stacked = parts[: len(parts) - j]
+        stacked = jnp.concatenate(stacked) if len(stacked) > 1 else stacked[0]
+        terms.append(lax.dot_general(stacked, piece, dims, preferred_element_type=jnp.float32))
+    total = None
+    for size in reversed(range(len(matrix))):
+        for j in range(size + 1):
+            i = size - j
+            term = terms[j][i * rows : (i + 1) * rows]
+            total = term if total is None else total + term
+    return total
 
 
 class Tables:
     def __init__(self, matrix_ref, ref, lanes, half):
         self.matrix_ref, self.ref, self.lanes, self.half = matrix_ref, ref, lanes, half
 
-    def inner(self):
-        return self.matrix_ref[: 2 * self.lanes, :]
-
-    def outer(self):
-        return self.matrix_ref[2 * self.lanes :, :]
+    def inner(self, parts):
+        return [self.matrix_ref[i * 3 * self.lanes : (i * 3 + 2) * self.lanes, :] for i in range(parts)]
+
+    def outer(self, h, parts):
+        part = slice(h * self.lanes, (h + 1) * self.lanes)
+        return [self.matrix_ref[(i * 3 + 2) * self.lanes : (i * 3 + 3) * self.lanes, part] for i in range(parts)]
 
     def decay(self):
         return self.ref[: self.half, :]
@@ -241,11 +271,10 @@
     main = real_forward(main)
     rim = real_forward([piece[:1, :] for piece in rim])
     edge[...] = jnp.zeros_like(edge)
+    left[...] = jnp.zeros_like(left)
     for h in range(2):
-        edge[:rows, h * lanes : (h + 1) * lanes] = main[h]
-        edge[rows : rows + 1, h * lanes : (h + 1) * lanes] = rim[h]
-        left[h, pl.ds(0, rows, stride=half), :] = main[h]
-        left[h, rows * half : rows * half + 1, :] = rim[h]
+        edge[h, :rows, :] = main[h]
+        edge[h, rows : rows + 1, :] = rim[h]
     for a in range(1, half):
         c, s = table.turn(a)
         for first, count, (re, im) in (
@@ -254,15 +283,12 @@
         ):
             left[0, pl.ds(first, count, stride=half), :] = re * c + im * s
             left[1, pl.ds(first, count, stride=half), :] = im * c - re * s
-    inner = jnp.dot(
-        jnp.concatenate([left[0], left[1]], axis=1), table.inner(), precision=highest, preferred_element_type=jnp.float32
-    )
-    outer = jnp.dot(edge[...], table.outer(), precision=highest, preferred_element_type=jnp.float32)
+    inner = product(jnp.concatenate([left[0], left[1]], axis=1), table.inner(3))
     for h in range(2):
-        part = slice(h * lanes, (h + 1) * lanes)
-        modes_ref[h, :, :] = inner[:, part]
-        modes_ref[h, pl.ds(0, rows, stride=half), :] = outer[:rows, part]
-        modes_ref[h, rows * half : rows * half + 1, :] = outer[rows : rows + 1, part]
+        modes_ref[h, :, :] = inner[: (rows + 1) * half, h * lanes : (h + 1) * lanes]
+        outer = product(edge[h], table.outer(h, 3))
+        modes_ref[h, pl.ds(0, rows, stride=half), :] = outer[:rows]
+        modes_ref[h, rows * half : rows * half + 1, :] = outer[rows : rows + 1]
     spectrum = row_list(modes_ref, rows, half)
     line = Line(table.decay(), rows, parts_y)
     below = line.low[0] * spectrum[0]
@@ -328,32 +354,27 @@
     edge[...] = jnp.zeros_like(edge)
     for i in reversed(range(rows + 1)):
         solved = gain * (line.high[i] * from_below[i] + line.low[i] * from_above)
-        edge[i : i + 1, :] = solved[:1, :]
-        for h in range(2):
-            left[h, i * half : (i + 1) * half, :] = solved[:, h * lanes : (h + 1) * lanes]
+        for h, sign in ((0, 1.0), (1, -1.0)):
+            part = solved[:, h * lanes : (h + 1) * lanes]
+            edge[h, i : i + 1, :] = part[:1, :]
+            left[h, i * half : (i + 1) * half, :] = sign * part
         from_above = line.step * (from_above + line.high[i] * spectrum[i])
-    back = (((1,), (1,)), ((), ()))
-    inner = lax.dot_general(
-        jnp.concatenate([left[0], left[1]], axis=1),
-        table.inner(),
-        back,
-        precision=highest,
-        preferred_element_type=jnp.float32,
-    )
-    outer = lax.dot_general(
-        edge[...], table.outer(), back, precision=highest, preferred_element_type=jnp.float32
-    )
+    left[:, (rows + 1) * half :, :] = jnp.zeros_like(left[:, (rows + 1) * half :, :])
+    inner = product(jnp.concatenate([left[0], left[1]], axis=1), table.inner(3))
+    main, rim = [], []
     for h in range(2):
         left[h, :, :] = inner[:, h * lanes : (h + 1) * lanes]
-    main = [outer[:rows, :lanes], outer[:rows, lanes:]] + [None] * (blocks - 2)
-    rim = [outer[rows : rows + 1, :lanes], outer[rows : rows + 1, lanes:]] + [None] * (blocks - 2)
+        outer = product(edge[h], table.outer(h, 3), transposed=True)
+        main.append(outer[:rows])
+        rim.append(outer[rows : rows + 1])
+    main, rim = main + [None] * (blocks - 2), rim + [None] * (blocks - 2)
     for a in range(1, half):
         c, s = table.turn(a)
         for planes, first, count in ((main, a, rows), (rim, rows * half + a, 1)):
             re = left[0, pl.ds(first, count, stride=half), :]
             im = left[1, pl.ds(first, count, stride=half), :]
-            planes[a + 1] = re * c - im * s
-            planes[half + a] = im * c + re * s
+            planes[a + 1] = re * c + im * s
+            planes[half + a] = re * s - im * c
     main, rim = real_inverse(main), real_inverse(rim)
     for d in range(blocks):
         ends = column_to_row(main[(d + 1) % blocks][:, :1], row, lane)
@@ -399,12 +420,15 @@
     message = shape_of(blocks, rows // 2 + 1, 2, cells)
     held = pltpu.VMEM((blocks, rows, cells), jnp.float32)
     room = pltpu.CompilerParams(vmem_limit_bytes=8 << 20)
-    scratch = [pltpu.VMEM((2, (rows + 1) * half, cells), jnp.float32), pltpu.VMEM((2 * rows, 2 * cells), jnp.float32)]
+    scratch = [
+        pltpu.VMEM((2, (rows + 2) * half, cells), jnp.float32),
+        pltpu.VMEM((2, 2 * rows, cells), jnp.float32),
+    ]
 
     kept = [matrices, *flat]
     sent, local, *kept = pl.pallas_call(
         functools.partial(source_kernel, planes, parts_y),
-        out_shape=(message, shape_of(2 * half, 2 * cells), *(shape_of(*a.shape) for a in kept)),
+        out_shape=(message, shape_of(2 * half, 2 * cells), *(jax.ShapeDtypeStruct(a.shape, a.dtype) for a in kept)),
         in_specs=[pl.BlockSpec(memory_space=pltpu.HBM)] * 5,
         scratch_shapes=[pltpu.SemaphoreType.DMA((6,))],
         compiler_params=room,

time: 73.2 us -> 72.8 us (level)
  no operation moved by 1% of the time
where the time goes in v6:
time: 72.8 us; the launch traced here: 72.5 us
  blocking collectives  68.8 us (95%)
  Pallas kernels  3.11 us (4%)
    all_to_all x2, blocking collectives, per_device(): taken = lax.all_to_all(sent, 'gx', 0, 0)  38.2 us
    all_to_all x1, blocking collectives, per_device(): taken = lax.all_to_all(sent, 'gy', 0, 0, axis_index_groups=far_groups)  18.8 us
    all_to_all x1, blocking collectives, per_device(): taken = lax.all_to_all(sent, 'gy', 0, 0, axis_index_groups=near_groups)  11.8 us

profile of v6, /device:TPU:1, one launch (start us, length us, event | category | flops | bytes accessed | tf_op | source)
XLA Modules:
  0.0 72.5 jit_solution(8850068569954150395)
XLA Ops:
  0.6 1.3 %source.1 = (f32[16,5,2,128]{3,2,1,0:T(2,128)S(1)}, f32[16,256]{1,0:T(8,128)S(1)}, bf16[1152,256]{1,0:T(8,128)(2,1)S(1)}, f32[128,128]{1,0:T(8,128)S(1)}, f32[12...) custom-call(f32[128,128]{1,0:T(8,128)} %bitcast.7, f32[128,128]{1,0:T(8,128)} %bitcast.8, f32[128,128]{1,0:T(8,128)} %bitcast.9, ...), custom_call_target="tpu_custom_call" | custom-call | tf_op jit(solution)/shard_map/source/pallas_call | solution.py:429
  1.9 24.7 %all_to_all.20.in_ref = f32[16,5,2,128]{3,2,1,0:T(2,128)S(1)} all-to-all(f32[16,5,2,128]{3,2,1,0:T(2,128)S(1)} %get-tuple-element.18), channel_id=1, replica_groups=mesh['gx'=16,'gy'=64] {'gx'}, dimensions={0} | all-to-all | bytes 163840 | tf_op jit(solution)/shard_map/all_to_all | solution.py:438
  26.6 0.4 modes.1
  27.1 11.8 %all_to_all.21.in_ref = f32[8,16,256]{2,1,0:T(8,128)S(1)} all-to-all(f32[8,16,256]{2,1,0:T(8,128)S(1)} %get-tuple-element.21), channel_id=1, replica_groups={{0,1,2,3,4,5,6,7},{8,9,10,11,12,13,14,15},{16,17,18,19,20,21,22,23},{24..., dimensions={0} | all-to-all | bytes 262144 | tf_op jit(solution)/shard_map/all_to_all | solution.py:446
  38.9 18.8 %all_to_all.22.in_ref = f32[8,8,256]{2,1,0:T(8,128)S(1)} all-to-all(f32[8,8,256]{2,1,0:T(8,128)S(1)} %get-tuple-element.22), channel_id=1, replica_groups={{0,8,16,24,32,40,48,56},{1,9,17,25,33,41,49,57},{2,10,18,26,34,42,50,58..., dimensions={0} | all-to-all | bytes 131072 | tf_op jit(solution)/shard_map/all_to_all | solution.py:453
  57.7 0.5 solve.1
  58.1 13.4 %all_to_all.23.in_ref = f32[16,5,2,128]{3,2,1,0:T(2,128)S(1)} all-to-all(f32[16,5,2,128]{3,2,1,0:T(2,128)S(1)} %solve.1), channel_id=1, replica_groups=mesh['gx'=16,'gy'=64] {'gx'}, dimensions={0} | all-to-all | bytes 163840 | tf_op jit(solution)/shard_map/all_to_all | solution.py:461
  71.6 0.9 %correct.1 = (f32[128,128]{1,0:T(8,128)}, f32[128,128]{1,0:T(8,128)}, f32[128,128]{1,0:T(8,128)}, f32[128,128]{1,0:T(8,128)}) custom-call(f32[16,5,2,128]{3,2,1,0:T(2,128)S(1)} %all_to_all.23.in_ref, f32[128,128]{1,0:T(8,128)S(1)} %get-tuple-element.25.stream_ref, f32[128,128]{1,0:T(8,128)S(1)} %get-tuple-element.26.normal_ref, ...), custom_call_target="tpu_custom_call" | custom-call | tf_op jit(solution)/shard_map/correct/pallas_call | solution.py:462
  (1 shorter events, 0.0 us)

commit v7 on v6

--- a/solution.py
+++ b/solution.py
@@ -3,7 +3,6 @@
 
 import jax
 import jax.numpy as jnp
-import ml_dtypes
 import numpy as np
 from jax import lax
 from jax.experimental import pallas as pl
@@ -98,11 +97,7 @@
     decay = decay.reshape(planes * half, 2 * lanes)
     turns = np.concatenate([turns[:half], turns[half:]], axis=1)
     matrices = np.concatenate([inner, outer])
-    parts = []
-    for _ in range(3):
-        parts.append(matrices.astype(ml_dtypes.bfloat16))
-        matrices = matrices - parts[-1].astype(np.float64)
-    return jnp.asarray(np.concatenate(parts)), jnp.asarray(np.concatenate([decay, turns]), jnp.float32)
+    return jnp.asarray(matrices, jnp.float32), jnp.asarray(np.concatenate([decay, turns]), jnp.float32)
 
 
 def split(values, count):
@@ -114,7 +109,7 @@
 
 
 def product(values, matrix, transposed=False):
-    parts, rows = split(values, len(matrix)), values.shape[0]
+    parts, matrix, rows = split(values, 3), split(matrix, 3), values.shape[0]
     dims = (((1,), (1 if transposed else 0,)), ((), ()))
     terms = []
     for j, piece in enumerate(matrix):
@@ -134,12 +129,11 @@
     def __init__(self, matrix_ref, ref, lanes, half):
         self.matrix_ref, self.ref, self.lanes, self.half = matrix_ref, ref, lanes, half
 
-    def inner(self, parts):
-        return [self.matrix_ref[i * 3 * self.lanes : (i * 3 + 2) * self.lanes, :] for i in range(parts)]
-
-    def outer(self, h, parts):
-        part = slice(h * self.lanes, (h + 1) * self.lanes)
-        return [self.matrix_ref[(i * 3 + 2) * self.lanes : (i * 3 + 3) * self.lanes, part] for i in range(parts)]
+    def inner(self):
+        return self.matrix_ref[: 2 * self.lanes, :]
+
+    def outer(self, h):
+        return self.matrix_ref[2 * self.lanes :, h * self.lanes : (h + 1) * self.lanes]
 
     def decay(self):
         return self.ref[: self.half, :]
@@ -283,10 +277,10 @@
         ):
             left[0, pl.ds(first, count, stride=half), :] = re * c + im * s
             left[1, pl.ds(first, count, stride=half), :] = im * c - re * s
-    inner = product(jnp.concatenate([left[0], left[1]], axis=1), table.inner(3))
+    inner = product(jnp.concatenate([left[0], left[1]], axis=1), table.inner())
     for h in range(2):
         modes_ref[h, :, :] = inner[: (rows + 1) * half, h * lanes : (h + 1) * lanes]
-        outer = product(edge[h], table.outer(h, 3))
+        outer = product(edge[h], table.outer(h))
         modes_ref[h, pl.ds(0, rows, stride=half), :] = outer[:rows]
         modes_ref[h, rows * half : rows * half + 1, :] = outer[rows : rows + 1]
     spectrum = row_list(modes_ref, rows, half)
@@ -360,11 +354,11 @@
             left[h, i * half : (i + 1) * half, :] = sign * part
         from_above = line.step * (from_above + line.high[i] * spectrum[i])
     left[:, (rows + 1) * half :, :] = jnp.zeros_like(left[:, (rows + 1) * half :, :])
-    inner = product(jnp.concatenate([left[0], left[1]], axis=1), table.inner(3))
+    inner = product(jnp.concatenate([left[0], left[1]], axis=1), table.inner())
     main, rim = [], []
     for h in range(2):
         left[h, :, :] = inner[:, h * lanes : (h + 1) * lanes]
-        outer = product(edge[h], table.outer(h, 3), transposed=True)
+        outer = product(edge[h], table.outer(h), transposed=True)
         main.append(outer[:rows])
         rim.append(outer[rows : rows + 1])
     main, rim = main + [None] * (blocks - 2), rim + [None] * (blocks - 2)

time: 72.8 us -> 72.8 us (level)
  no operation moved by 1% of the time
where the time goes in v7:
time: 72.8 us; the launch traced here: 72.5 us
  blocking collectives  68.8 us (95%)
  Pallas kernels  3.06 us (4%)
    all_to_all x2, blocking collectives, per_device(): taken = lax.all_to_all(sent, 'gx', 0, 0)  38.2 us
    all_to_all x1, blocking collectives, per_device(): taken = lax.all_to_all(sent, 'gy', 0, 0, axis_index_groups=far_groups)  18.8 us
    all_to_all x1, blocking collectives, per_device(): taken = lax.all_to_all(sent, 'gy', 0, 0, axis_index_groups=near_groups)  11.8 us

profile of v7, /device:TPU:1, one launch (start us, length us, event | category | flops | bytes accessed | tf_op | source)
XLA Modules:
  0.0 72.5 jit_solution(3804878149030717762)
XLA Ops:
  0.6 1.2 %source.1 = (f32[16,5,2,128]{3,2,1,0:T(2,128)S(1)}, f32[16,256]{1,0:T(8,128)S(1)}, f32[384,256]{1,0:T(8,128)S(1)}, f32[128,128]{1,0:T(8,128)S(1)}, f32[128,128]{1,0:T(8,128)S(1)}, /*index=5*/f32[128,128]{1,0:T(8,128)S(1)}) custom-call(f32[128,128]{1,0:T(8,128)} %bitcast.7, f32[128,128]{1,0:T(8,128)} %bitcast.8, f32[128,128]{1,0:T(8,128)} %bitcast.9, ...), custom_call_target="tpu_custom_call" | custom-call | tf_op jit(solution)/shard_map/source/pallas_call | solution.py:423
  1.8 24.7 %all_to_all.20.in_ref = f32[16,5,2,128]{3,2,1,0:T(2,128)S(1)} all-to-all(f32[16,5,2,128]{3,2,1,0:T(2,128)S(1)} %get-tuple-element.18), channel_id=1, replica_groups=mesh['gx'=16,'gy'=64] {'gx'}, dimensions={0} | all-to-all | bytes 163840 | tf_op jit(solution)/shard_map/all_to_all | solution.py:432
  26.6 0.4 modes.1
  27.0 11.8 %all_to_all.21.in_ref = f32[8,16,256]{2,1,0:T(8,128)S(1)} all-to-all(f32[8,16,256]{2,1,0:T(8,128)S(1)} %get-tuple-element.21), channel_id=1, replica_groups={{0,1,2,3,4,5,6,7},{8,9,10,11,12,13,14,15},{16,17,18,19,20,21,22,23},{24..., dimensions={0} | all-to-all | bytes 262144 | tf_op jit(solution)/shard_map/all_to_all | solution.py:440
  38.8 18.8 %all_to_all.22.in_ref = f32[8,8,256]{2,1,0:T(8,128)S(1)} all-to-all(f32[8,8,256]{2,1,0:T(8,128)S(1)} %get-tuple-element.22), channel_id=1, replica_groups={{0,8,16,24,32,40,48,56},{1,9,17,25,33,41,49,57},{2,10,18,26,34,42,50,58..., dimensions={0} | all-to-all | bytes 131072 | tf_op jit(solution)/shard_map/all_to_all | solution.py:447
  57.6 0.5 solve.1
  58.1 13.4 %all_to_all.23.in_ref = f32[16,5,2,128]{3,2,1,0:T(2,128)S(1)} all-to-all(f32[16,5,2,128]{3,2,1,0:T(2,128)S(1)} %solve.1), channel_id=1, replica_groups=mesh['gx'=16,'gy'=64] {'gx'}, dimensions={0} | all-to-all | bytes 163840 | tf_op jit(solution)/shard_map/all_to_all | solution.py:455
  71.5 0.9 %correct.1 = (f32[128,128]{1,0:T(8,128)}, f32[128,128]{1,0:T(8,128)}, f32[128,128]{1,0:T(8,128)}, f32[128,128]{1,0:T(8,128)}) custom-call(f32[16,5,2,128]{3,2,1,0:T(2,128)S(1)} %all_to_all.23.in_ref, f32[128,128]{1,0:T(8,128)S(1)} %get-tuple-element.25.stream_ref, f32[128,128]{1,0:T(8,128)S(1)} %get-tuple-element.26.normal_ref, ...), custom_call_target="tpu_custom_call" | custom-call | tf_op jit(solution)/shard_map/correct/pallas_call | solution.py:456
  (1 shorter events, 0.0 us)

commit v8 on v7

--- a/solution.py
+++ b/solution.py
@@ -62,6 +62,16 @@
         values[i] = even + odd
         values[count - i] = even - odd
     return values
+
+
+def halves_apart(count):
+    order = [i // 2 + i % 2 * (count // 2) for i in range(count)]
+    return order, [order.index(i) for i in range(count)]
+
+
+def evens_first(count):
+    order = [*range(0, count, 2), *range(1, count, 2)]
+    return order, [order.index(i) for i in range(count)]
 
 
 def plane_modes(count):
@@ -177,7 +187,9 @@
     done,
 ):
     half = local_ref.shape[0] // 2
-    decay_rows = pl.ds(pl.multiple_of(lax.axis_index("gx") * half, half), half)
+    index = lax.axis_index("gx")
+    plane_here = lax.rem(index, 2) * (planes // 2) + lax.div(index, 2)
+    decay_rows = pl.ds(pl.multiple_of(plane_here * half, half), half)
     turn_rows = pl.ds(table_hbm.shape[0] - half, half)
     copies = [
         pltpu.make_async_copy(stream_hbm, stream_ref, done.at[0]),
@@ -259,6 +271,8 @@
     table = Tables(matrix_ref, table_ref, lanes, half)
     row, lane = places((rows, lanes))
     main, rim = take(in_ref, held)
+    spot = evens_first(blocks)[1]
+    main, rim = [main[spot[d]] for d in range(blocks)], [rim[spot[d]] for d in range(blocks)]
     for d in range(blocks):
         ends = row_to_column(rim[d - 1][1:2, :], row, lane)
         main[d] = main[d] + jnp.where(lane == 0, ends, 0.0)
@@ -307,23 +321,25 @@
     step = jnp.exp(-rows * table_ref[:half, :])
     place, group = lax.rem(lax.axis_index("gy"), near), lax.div(lax.axis_index("gy"), near)
     below = above = jnp.zeros_like(step)
+    spot = halves_apart(near)[1]
     for i in range(near):
         j = near - 1 - i
         mine_ref[:half, :] = jnp.where(place == i, below, mine_ref[:half, :]) if i else below
         mine_ref[half:, :] = jnp.where(place == j, above, mine_ref[half:, :]) if i else above
-        below = in_ref[i, :half, :] + step * below
-        above = in_ref[j, half:, :] + step * above
-    for other in range(send_ref.shape[0]):
-        send_ref[other, :, :] = jnp.where(group < other, below, above)
+        below = in_ref[spot[i], :half, :] + step * below
+        above = in_ref[spot[j], half:, :] + step * above
+    for i, other in enumerate(halves_apart(send_ref.shape[0])[0]):
+        send_ref[i, :, :] = jnp.where(group < other, below, above)
 
 
 def entering(pieces_ref, mine, step):
     count = pieces_ref.shape[0]
+    spot = halves_apart(count)[1]
     below = above = jnp.zeros_like(step)
     for i in range(count):
         j = count - 1 - i
-        below = jnp.where(i < mine, pieces_ref[i] + step * below, below)
-        above = jnp.where(j > mine, pieces_ref[j] + step * above, above)
+        below = jnp.where(i < mine, pieces_ref[spot[i]] + step * below, below)
+        above = jnp.where(j > mine, pieces_ref[spot[j]] + step * above, above)
     return below, above
 
 
@@ -370,9 +386,10 @@
             planes[a + 1] = re * c + im * s
             planes[half + a] = re * s - im * c
     main, rim = real_inverse(main), real_inverse(rim)
+    spot = evens_first(blocks)[1]
     for d in range(blocks):
         ends = column_to_row(main[(d + 1) % blocks][:, :1], row, lane)
-        put(out_ref, d, main[d], jnp.where(row == 0, rim[d], ends))
+        put(out_ref, spot[d], main[d], jnp.where(row == 0, rim[d], ends))
 
 
 def correct_kernel(
@@ -408,8 +425,8 @@
     if planes != parts_x or rows != half or near * far != parts_y:
         raise ValueError("unsupported sizes")
     matrices, table = tables(planes, cells, blocks, cells * parts_x)
-    near_groups = [[i * near + k for k in range(near)] for i in range(far)]
-    far_groups = [[i + k * near for k in range(far)] for i in range(near)]
+    near_groups = [[i * near + k for k in halves_apart(near)[0]] for i in range(far)]
+    far_groups = [[i + k * near for k in halves_apart(far)[0]] for i in range(near)]
     flat = [a.reshape(rows * planes, cells) for a in (stream_vel, normal_vel, span_vel)]
     message = shape_of(blocks, rows // 2 + 1, 2, cells)
     held = pltpu.VMEM((blocks, rows, cells), jnp.float32)
@@ -429,7 +446,7 @@
         name="source",
     )(*(pltpu.with_memory_space_constraint(a, pltpu.HBM) for a in (*flat, table, matrices)))
     matrices, *flat = kept
-    taken = lax.all_to_all(sent, "gx", 0, 0)
+    taken = lax.all_to_all(sent, "gx", 0, 0, axis_index_groups=[evens_first(blocks)[0]])
     sent, modes = pl.pallas_call(
         functools.partial(modes_kernel, rows, parts_y),
         out_shape=(shape_of(near, 2 * half, 2 * cells), shape_of(2, (rows + 1) * half, cells)),
@@ -452,7 +469,7 @@
         compiler_params=room,
         name="solve",
     )(taken, mine, modes, matrices, local)
-    taken = lax.all_to_all(sent, "gx", 0, 0)
+    taken = lax.all_to_all(sent, "gx", 0, 0, axis_index_groups=[evens_first(blocks)[0]])
     outs = pl.pallas_call(
         functools.partial(correct_kernel, parts_y),
         out_shape=(shape_of(rows * planes, cells),) * 4,

time: 72.8 us -> 69.7 us (0.957)
  blocking collectives: 68.8 us -> 65.7 us
    all_to_all x1, blocking collectives: 11.8 us -> 9.18 us  [per_device(): taken = lax.all_to_all(sent, 'gy', 0, 0, axis_index_groups=near_groups)]
where the time goes in v8:
time: 69.7 us; the launch traced here: 69.4 us
  blocking collectives  65.7 us (94%)
  Pallas kernels  3.06 us (4%)
    all_to_all x2, blocking collectives, per_device(): lax.all_to_all(sent, 'gx', 0, 0, axis_index_groups=[evens_first(blocks)[0]])  37.5 us
    all_to_all x1, blocking collectives, per_device(): taken = lax.all_to_all(sent, 'gy', 0, 0, axis_index_groups=far_groups)  19 us
    all_to_all x1, blocking collectives, per_device(): taken = lax.all_to_all(sent, 'gy', 0, 0, axis_index_groups=near_groups)  9.18 us

profile of v8, /device:TPU:1, one launch (start us, length us, event | category | flops | bytes accessed | tf_op | source)
XLA Modules:
  0.0 69.4 jit_solution(17620957461575317777)
XLA Ops:
  0.6 1.2 %source.1 = (f32[16,5,2,128]{3,2,1,0:T(2,128)S(1)}, f32[16,256]{1,0:T(8,128)S(1)}, f32[384,256]{1,0:T(8,128)S(1)}, f32[128,128]{1,0:T(8,128)S(1)}, f32[128,128]{1,0:T(8,128)S(1)}, /*index=5*/f32[128,128]{1,0:T(8,128)S(1)}) custom-call(f32[128,128]{1,0:T(8,128)} %bitcast.7, f32[128,128]{1,0:T(8,128)} %bitcast.8, f32[128,128]{1,0:T(8,128)} %bitcast.9, ...), custom_call_target="tpu_custom_call" | custom-call | tf_op jit(solution)/shard_map/source/pallas_call | solution.py:440
  1.8 23.9 %all_to_all.20.in_ref = f32[16,5,2,128]{3,2,1,0:T(2,128)S(1)} all-to-all(f32[16,5,2,128]{3,2,1,0:T(2,128)S(1)} %get-tuple-element.18), channel_id=1, replica_groups={{0,128,256,384,512,640,768,896,64,192,320,448,576,704,832,960},{1,129,2..., dimensions={0} | all-to-all | bytes 163840 | tf_op jit(solution)/shard_map/all_to_all | solution.py:449
  25.7 0.4 modes.1
  26.1 9.2 %all_to_all.21.in_ref = f32[8,16,256]{2,1,0:T(8,128)S(1)} all-to-all(f32[8,16,256]{2,1,0:T(8,128)S(1)} %get-tuple-element.21), channel_id=1, replica_groups={{0,4,1,5,2,6,3,7},{8,12,9,13,10,14,11,15},{16,20,17,21,18,22,19,23},{24..., dimensions={0} | all-to-all | bytes 262144 | tf_op jit(solution)/shard_map/all_to_all | solution.py:457
  35.3 19.0 %all_to_all.22.in_ref = f32[8,8,256]{2,1,0:T(8,128)S(1)} all-to-all(f32[8,8,256]{2,1,0:T(8,128)S(1)} %get-tuple-element.22), channel_id=1, replica_groups={{0,32,8,40,16,48,24,56},{1,33,9,41,17,49,25,57},{2,34,10,42,18,50,26,58..., dimensions={0} | all-to-all | bytes 131072 | tf_op jit(solution)/shard_map/all_to_all | solution.py:464
  54.4 0.5 solve.1
  54.8 13.6 %all_to_all.23.in_ref = f32[16,5,2,128]{3,2,1,0:T(2,128)S(1)} all-to-all(f32[16,5,2,128]{3,2,1,0:T(2,128)S(1)} %solve.1), channel_id=1, replica_groups={{0,128,256,384,512,640,768,896,64,192,320,448,576,704,832,960},{1,129,2..., dimensions={0} | all-to-all | bytes 163840 | tf_op jit(solution)/shard_map/all_to_all | solution.py:472
  68.4 0.9 %correct.1 = (f32[128,128]{1,0:T(8,128)}, f32[128,128]{1,0:T(8,128)}, f32[128,128]{1,0:T(8,128)}, f32[128,128]{1,0:T(8,128)}) custom-call(f32[16,5,2,128]{3,2,1,0:T(2,128)S(1)} %all_to_all.23.in_ref, f32[128,128]{1,0:T(8,128)S(1)} %get-tuple-element.25.stream_ref, f32[128,128]{1,0:T(8,128)S(1)} %get-tuple-element.26.normal_ref, ...), custom_call_target="tpu_custom_call" | custom-call | tf_op jit(solution)/shard_map/correct/pallas_call | solution.py:473
  (1 shorter events, 0.0 us)

commit v9 on v8

--- a/solution.py
+++ b/solution.py
@@ -70,7 +70,7 @@
 
 
 def evens_first(count):
-    order = [*range(0, count, 2), *range(1, count, 2)]
+    order = [2 * i + odd for odd in range(2) for i in halves_apart(count // 2)[0]]
     return order, [order.index(i) for i in range(count)]
 
 
@@ -188,7 +188,8 @@
 ):
     half = local_ref.shape[0] // 2
     index = lax.axis_index("gx")
-    plane_here = lax.rem(index, 2) * (planes // 2) + lax.div(index, 2)
+    chip, quarter = lax.div(index, 2), planes // 4
+    plane_here = lax.rem(index, 2) * (planes // 2) + 2 * lax.rem(chip, quarter) + lax.div(chip, quarter)
     decay_rows = pl.ds(pl.multiple_of(plane_here * half, half), half)
     turn_rows = pl.ds(table_hbm.shape[0] - half, half)
     copies = [

time: 69.7 us -> 70.5 us (1.011)
  blocking collectives: 65.7 us -> 66.5 us
    all_to_all x2, blocking collectives: 37.5 us -> 38.3 us  [per_device(): lax.all_to_all(sent, 'gx', 0, 0, axis_index_groups=[evens_first(blocks)[0]])]
where the time goes in v9:
time: 70.5 us; the launch traced here: 70.2 us
  blocking collectives  66.5 us (94%)
  Pallas kernels  3.06 us (4%)
    all_to_all x2, blocking collectives, per_device(): lax.all_to_all(sent, 'gx', 0, 0, axis_index_groups=[evens_first(blocks)[0]])  38.3 us
    all_to_all x1, blocking collectives, per_device(): taken = lax.all_to_all(sent, 'gy', 0, 0, axis_index_groups=far_groups)  19.1 us
    all_to_all x1, blocking collectives, per_device(): taken = lax.all_to_all(sent, 'gy', 0, 0, axis_index_groups=near_groups)  9.11 us

profile of v9, /device:TPU:1, one launch (start us, length us, event | category | flops | bytes accessed | tf_op | source)
XLA Modules:
  0.0 70.2 jit_solution(12673998278153421814)
XLA Ops:
  0.6 1.2 %source.1 = (f32[16,5,2,128]{3,2,1,0:T(2,128)S(1)}, f32[16,256]{1,0:T(8,128)S(1)}, f32[384,256]{1,0:T(8,128)S(1)}, f32[128,128]{1,0:T(8,128)S(1)}, f32[128,128]{1,0:T(8,128)S(1)}, /*index=5*/f32[128,128]{1,0:T(8,128)S(1)}) custom-call(f32[128,128]{1,0:T(8,128)} %bitcast.7, f32[128,128]{1,0:T(8,128)} %bitcast.8, f32[128,128]{1,0:T(8,128)} %bitcast.9, ...), custom_call_target="tpu_custom_call" | custom-call | tf_op jit(solution)/shard_map/source/pallas_call | solution.py:441
  1.8 24.3 %all_to_all.20.in_ref = f32[16,5,2,128]{3,2,1,0:T(2,128)S(1)} all-to-all(f32[16,5,2,128]{3,2,1,0:T(2,128)S(1)} %get-tuple-element.18), channel_id=1, replica_groups={{0,512,128,640,256,768,384,896,64,576,192,704,320,832,448,960},{1,513,1..., dimensions={0} | all-to-all | bytes 163840 | tf_op jit(solution)/shard_map/all_to_all | solution.py:450
  26.2 0.4 modes.1
  26.6 9.1 %all_to_all.21.in_ref = f32[8,16,256]{2,1,0:T(8,128)S(1)} all-to-all(f32[8,16,256]{2,1,0:T(8,128)S(1)} %get-tuple-element.21), channel_id=1, replica_groups={{0,4,1,5,2,6,3,7},{8,12,9,13,10,14,11,15},{16,20,17,21,18,22,19,23},{24..., dimensions={0} | all-to-all | bytes 262144 | tf_op jit(solution)/shard_map/all_to_all | solution.py:458
  35.7 19.1 %all_to_all.22.in_ref = f32[8,8,256]{2,1,0:T(8,128)S(1)} all-to-all(f32[8,8,256]{2,1,0:T(8,128)S(1)} %get-tuple-element.22), channel_id=1, replica_groups={{0,32,8,40,16,48,24,56},{1,33,9,41,17,49,25,57},{2,34,10,42,18,50,26,58..., dimensions={0} | all-to-all | bytes 131072 | tf_op jit(solution)/shard_map/all_to_all | solution.py:465
  54.8 0.5 solve.1
  55.3 14.0 %all_to_all.23.in_ref = f32[16,5,2,128]{3,2,1,0:T(2,128)S(1)} all-to-all(f32[16,5,2,128]{3,2,1,0:T(2,128)S(1)} %solve.1), channel_id=1, replica_groups={{0,512,128,640,256,768,384,896,64,576,192,704,320,832,448,960},{1,513,1..., dimensions={0} | all-to-all | bytes 163840 | tf_op jit(solution)/shard_map/all_to_all | solution.py:473
  69.3 0.9 %correct.1 = (f32[128,128]{1,0:T(8,128)}, f32[128,128]{1,0:T(8,128)}, f32[128,128]{1,0:T(8,128)}, f32[128,128]{1,0:T(8,128)}) custom-call(f32[16,5,2,128]{3,2,1,0:T(2,128)S(1)} %all_to_all.23.in_ref, f32[128,128]{1,0:T(8,128)S(1)} %get-tuple-element.25.stream_ref, f32[128,128]{1,0:T(8,128)S(1)} %get-tuple-element.26.normal_ref, ...), custom_call_target="tpu_custom_call" | custom-call | tf_op jit(solution)/shard_map/correct/pallas_call | solution.py:474
  (1 shorter events, 0.0 us)
